TPU v7x, 256 devices: a whole 4x4x8 slice. The times are simulated.
256 devices in a mesh: clus: 32 (over x, z), sub: 8 (over y, core).
Axes of the slice: x: 4, y: 4, z: 8, core: 2. Of those that a mesh axis runs over, the one named last changes fastest.
Arguments:
- forward_rhs: bfloat16 [1024, 32, 256], P('clus', 'sub'), may hold values from -6 to 6
- adjoint_rhs: bfloat16 [1024, 32, 256], P('clus', 'sub'), may hold values from -6 to 6
- far_clusters: int32 [2, 32768], P(None, ('clus', 'sub')), may hold values from 0 to 1023, as said below
- far_ranks: int32 [32768], P(('clus', 'sub')), may hold values from 0 to 32, as said below
- far_left: bfloat16 [32768, 2, 32, 128], P(('clus', 'sub')), may hold values from -0.25 to 0.25
- far_right: bfloat16 [32768, 2, 32, 128], P(('clus', 'sub')), may hold values from -0.5 to 0.5
- near_clusters: int32 [2, 8192], P(None, ('clus', 'sub')), may hold values from 0 to 1023, as said below
- near_blocks: bfloat16 [8192, 2, 128, 128], P(('clus', 'sub')), may hold values from -0.125 to 0.125
- panel_params: int32 [4, 131072], P(None, 'clus'), may hold values from 0 to 32767, as said below
- panel_weights: float32 [4, 131072], P(None, 'clus'), may hold values from -6 to 6
- panel_counts: int32 [131072], P('clus'), may hold values from 1 to 4
Outputs:
- forward_field: float32 [1024, 32, 256], P('clus', 'sub')
- adjoint_field: float32 [1024, 32, 256], P('clus', 'sub')
- param_gradient: float32 [32768], P(('clus', 'sub'))
Inputs may be any that keep to these rules, and one draw needn't show every extreme that they name: `far_clusters`: block slot b belongs to device b // 128; its row cluster lies in row group g = (b // 128) // 8, among clusters 32 * g to 32 * g + 31; its column cluster is the row cluster plus d modulo 1024 with 2 <= |d| <= 32. `far_ranks`: 0 marks an empty slot; on each device the live slots come first. `near_clusters`: block slot b belongs to device b // 32; its row cluster lies in row group (b // 32) // 8; its column cluster is the row cluster plus d modulo 1024 with |d| <= 1. panel_params[0,p] equals p // 4 plus an offset of -3 to 3, modulo 32768; the other slots may name any shape parameter.
All inputs are finite; a program needn't handle non-finite values.
Results may differ from a plain program's by a relative error of at most 0.0036.
Values may be sent and summed in bfloat16 or wider, within the bound.
A program may use at most 128 MiB of HBM per device.

v0:
```python
import jax
import jax.numpy as jnp
from jax import lax
from jax.sharding import PartitionSpec as P

PAR_DEV = 128


def extended(x, sides, width):
    for axis, dim in sides:
        devices, length = (lax.axis_size(axis), x.shape[dim])
        up = [(i, (i + 1) % devices) for i in range(devices)]
        down = [(j, i) for i, j in up]
        last = lax.slice_in_dim(x, length - width, length, axis=dim)
        leading = lax.slice_in_dim(x, 0, width, axis=dim)
        before = lax.ppermute(last, axis, up)
        after = lax.ppermute(leading, axis, down)
        x = jnp.concatenate([before, x, after], axis=dim)
    return x


def shifted(x, axis, by):
    devices = lax.axis_size(axis)
    return lax.ppermute(x, axis, [(i, (i + by) % devices) for i in range(devices)])


def complex_mix(lhs_data, rhs_factor, einsum_form):
    width = lhs_data.shape[-1] // 2
    real_lhs = lhs_data[..., :width]
    imag_lhs = lhs_data[..., width:]
    real_rhs = rhs_factor[:, 0]
    imag_rhs = rhs_factor[:, 1]
    real_out = jnp.einsum(
        einsum_form, real_lhs, real_rhs, preferred_element_type=jnp.float32
    ) - jnp.einsum(einsum_form, imag_lhs, imag_rhs, preferred_element_type=jnp.float32)
    imag_out = jnp.einsum(
        einsum_form, real_lhs, imag_rhs, preferred_element_type=jnp.float32
    ) + jnp.einsum(einsum_form, imag_lhs, real_rhs, preferred_element_type=jnp.float32)
    return jnp.concatenate([real_out, imag_out], axis=-1)


def rank_columns(rank_list, width):
    column_ids = lax.broadcasted_iota(jnp.int32, (rank_list.shape[0], width), 1)
    kept = (column_ids < rank_list[:, None]).astype(jnp.float32)
    return jnp.concatenate([kept, kept], axis=1)[:, None, :]


def shards(
    forward_rhs,
    adjoint_rhs,
    far_clusters,
    far_ranks,
    far_left,
    far_right,
    near_clusters,
    near_blocks,
    panel_params,
    panel_weights,
    panel_counts,
):
    groups = lax.axis_size("clus")
    members = lax.axis_size("sub")
    clusters = forward_rhs.shape[0]
    total_clusters = clusters * groups
    first_cluster = lax.axis_index("clus") * clusters
    whole_rhs, whole_adj = (
        lax.all_gather(forward_rhs, "sub", axis=1, tiled=True),
        lax.all_gather(adjoint_rhs, "sub", axis=1, tiled=True),
    )
    widened = extended(whole_rhs, (("clus", 0),), clusters)
    far_rows = far_clusters[0] - first_cluster
    far_cols = (far_clusters[1] - first_cluster + clusters) % total_clusters
    near_rows = near_clusters[0] - first_cluster
    near_cols = (near_clusters[1] - first_cluster + clusters) % total_clusters
    rank_keep = rank_columns(far_ranks, far_left.shape[2])
    adj_far = jnp.take(whole_adj, far_rows, axis=0)
    coeff_adj = (complex_mix(adj_far, far_left, "bkp,bjp->bkj") * rank_keep).astype(jnp.bfloat16)
    far_back = complex_mix(coeff_adj, far_right, "bkj,bjq->bkq")
    near_back = complex_mix(jnp.take(whole_adj, near_rows, axis=0), near_blocks, "bkp,bpq->bkq")
    wide_back = jax.ops.segment_sum(
        far_back, far_cols, num_segments=3 * clusters
    ) + jax.ops.segment_sum(near_back, near_cols, num_segments=3 * clusters)
    rhs_far = jnp.take(widened, far_cols, axis=0)
    coeff_fwd = (complex_mix(rhs_far, far_right, "bkq,bjq->bkj") * rank_keep).astype(jnp.bfloat16)
    far_out = complex_mix(coeff_fwd, far_left, "bkj,bjp->bkp")
    near_out = complex_mix(jnp.take(widened, near_cols, axis=0), near_blocks, "bkq,bpq->bkp")
    forward_part = jax.ops.segment_sum(
        far_out, far_rows, num_segments=clusters
    ) + jax.ops.segment_sum(near_out, near_rows, num_segments=clusters)
    forward_field = lax.psum_scatter(forward_part, "sub", scatter_dimension=1, tiled=True)
    from_right = shifted(wide_back[:clusters], "clus", -1)
    from_left = shifted(wide_back[2 * clusters :], "clus", 1)
    own_terms = wide_back[clusters : 2 * clusters] + from_right + from_left
    adjoint_field = lax.psum_scatter(own_terms, "sub", scatter_dimension=1, tiled=True)
    half_width = forward_field.shape[-1] // 2
    column_total = forward_rhs.shape[1] * members
    sensitivity = (
        jnp.sum(
            forward_field[..., :half_width] * adjoint_field[..., :half_width]
            - forward_field[..., half_width:] * adjoint_field[..., half_width:],
            axis=1,
        ).reshape(-1)
        / column_total
    )
    param_total = PAR_DEV * groups * members
    slot_ids = lax.broadcasted_iota(jnp.int32, panel_params.shape, 0)
    live_slots = slot_ids < panel_counts[None, :]
    weighted = jnp.where(
        live_slots,
        panel_weights * sensitivity[None, :],
        jnp.zeros(panel_weights.shape, jnp.float32),
    )
    param_gradient = lax.psum_scatter(
        jax.ops.segment_sum(
            weighted.reshape(-1), panel_params.reshape(-1), num_segments=param_total
        ),
        ("clus", "sub"),
        scatter_dimension=0,
        tiled=True,
    )
    return (forward_field, adjoint_field, param_gradient)


def solution(mesh):
    in_specs = (
        P("clus", "sub", None),
        P("clus", "sub", None),
        P(None, ("clus", "sub")),
        P(("clus", "sub")),
        P(("clus", "sub"), None, None, None),
        P(("clus", "sub"), None, None, None),
        P(None, ("clus", "sub")),
        P(("clus", "sub"), None, None, None),
        P(None, "clus"),
        P(None, "clus"),
        P("clus"),
    )
    out_specs = (P("clus", "sub", None), P("clus", "sub", None), P(("clus", "sub")))
    return jax.shard_map(shards, mesh=mesh, in_specs=in_specs, out_specs=out_specs, check_vma=False)
```

profile of v0, /device:TPU:1, one launch (start us, length us, event | category | flops | bytes accessed | tf_op | source)
XLA Modules:
  0.0 561.8 jit_solution(7387840832901598644)
XLA Ops:
  8.1 16.1 %all_gather.6 = bf16[32,32,256]{2,0,1:T(8,128)(2,1)S(1)} all-gather(bf16[32,4,256]{2,0,1:T(8,128)(2,1)S(1)} %copy.38), channel_id=1, replica_groups=mesh['clus'=32,'sub'=8] {'sub'}, dimensions={1}, use_global_device_ids=true | all-gather | bytes 589824 | tf_op jit(solution)/shard_map/all_gather | solution.py:67
  25.8 6.1 %collective-permute-start.1 = (bf16[32,32,256]{2,1,0:T(8,128)(2,1)}, bf16[32,32,256]{2,1,0:T(8,128)(2,1)}, u32[]{:S(2)}, u32[]{:S(2)}) collective-permute-start(bf16[32,32,256]{2,1,0:T(8,128)(2,1)} %copy.39), channel_id=1, source_target_pairs={{8,0},{16,8},{24,16},{32,24},{40,32},{48,40},{56,48},{64,56},{72,6... | collective-permute-start | bytes 1572872 | tf_op jit(solution)/shard_map/ppermute | solution.py:17
  35.1 13.4 %all_gather.7 = bf16[32,32,256]{2,0,1:T(8,128)(2,1)S(1)} all-gather(bf16[32,4,256]{2,0,1:T(8,128)(2,1)S(1)} %copy.49), channel_id=1, replica_groups=mesh['clus'=32,'sub'=8] {'sub'}, dimensions={1}, use_global_device_ids=true | all-gather | bytes 589824 | tf_op jit(solution)/shard_map/all_gather | solution.py:68
  51.0 2.1 fusion.22
  53.1 2.0 fusion.15
  59.3 4.1 convolution_subtract_fusion.1
  63.4 2.0 convolution_add_fusion.1
  67.4 2.1 broadcast.357.clone.1
  69.4 5.6 scatter_fusion.3
  80.1 3.4 gather_fusion
  83.5 2.0 broadcast_select_fusion.1
  98.5 2.8 gather_fusion.1
  111.0 2.4 pad_maximum_fusion
  114.6 13.5 %scatter_fusion = f32[32,32,256]{2,1,0:T(8,128)S(1)} fusion(f32[32,32,256]{2,1,0:T(8,128)S(1)} %broadcast.352.clone, s32[128]{0:T(128)S(1)} %fusion.99, f32[128,32,256]{2,1,0:T(8,128)} %pad_maximum_fusion), kind=kCustom, calls=%fused_computation.4 | custom fusion | flops 1048576 | bytes 12583424 | tf_op jit(solution)/shard_map/scatter-add | solution.py:87
  128.2 3.8 scatter_fusion.1
  134.1 2.2 convolution_add_fusion
  136.4 2.4 pad_maximum_fusion.1
  139.2 13.5 %scatter_fusion.2 = f32[96,32,256]{2,1,0:T(8,128)S(1)} fusion(f32[96,32,256]{2,1,0:T(8,128)S(1)} %broadcast.357.clone, s32[128]{0:T(128)S(1)} %bitcast.106, f32[128,32,256]{2,1,0:T(8,128)} %pad_maximum_fusion.1), kind=kCustom, calls=%fused_computation.6 | custom fusion | flops 1048576 | bytes 12583424 | tf_op jit(solution)/shard_map/scatter-add | solution.py:80
  152.7 2.6 add.257
  157.2 22.8 %collective-permute-done.2 = f32[32,32,256]{2,1,0:T(8,128)S(1)} collective-permute-done((f32[32,32,256]{2,1,0:T(8,128)S(1)}, f32[32,32,256]{2,1,0:T(8,128)S(1)}, u32[]{:S(2)}, u32[]{:S(2)}) %collective-permute-start.2) | collective-permute-done | bytes 1048608 | tf_op jit(solution)/shard_map/ppermute | solution.py:24
  180.0 4.9 collective-permute-done.3
  186.9 26.8 %reduce-scatter.5.cloned.1.call-done = f32[32,4,256]{2,0,1:T(8,128)} async-done(((f32[32,32,256]{2,0,1:T(8,128)}), f32[32,4,256]{2,0,1:T(8,128)}) %reduce-scatter.5.cloned.1.call-update) | async-done | bytes 131088 | tf_op jit(solution)/shard_map/reduce_scatter | solution.py:94
  214.8 93.3 %scatter_custom_fusion.4 = f32[32768]{0:T(1024)} fusion(s32[16384]{0:T(1024)S(1)} %bitcast.104, f32[16384]{0:T(1024)S(1)} %bitcast.105, f32[]{:T(128)} %constant.86.clone.1), kind=kCustom, calls=%fused_computation.125 | custom fusion | flops 16384 | bytes 131076 | tf_op jit(solution)/shard_map/scatter-add | solution.py:114
  311.4 242.6 %all-reduce.3.cloned.1.call-done = f32[32768]{0:T(1024)} async-done(((f32[32768]{0:T(1024)}), f32[32768]{0:T(1024)}) %all-reduce.3.cloned.1.call-update) | async-done | bytes 131088
  (122 shorter events, 55.1 us)
Async XLA Ops:
  7.2 179.7 %reduce-scatter.3.cloned.1.call-start = ((), (), s32[]{:S(2)}) async-start(), calls=%async_computation.2 | async-start | bytes 1179648 | tf_op jit(solution)/shard_map/reduce_scatter | solution.py:90
  25.3 49.8 %collective-permute-start = (bf16[32,32,256]{2,1,0:T(8,128)(2,1)}, bf16[32,32,256]{2,1,0:T(8,128)(2,1)}, u32[]{:S(2)}, u32[]{:S(2)}) collective-permute-start(bf16[32,32,256]{2,1,0:T(8,128)(2,1)} %copy.39), channel_id=1, source_target_pairs={{0,8},{8,16},{16,24},{24,32},{32,40},{40,48},{48,56},{56,64},{64,7... | collective-permute-start | bytes 1572872 | tf_op jit(solution)/shard_map/ppermute | solution.py:16
  25.8 52.4 %collective-permute-start.1 = (bf16[32,32,256]{2,1,0:T(8,128)(2,1)}, bf16[32,32,256]{2,1,0:T(8,128)(2,1)}, u32[]{:S(2)}, u32[]{:S(2)}) collective-permute-start(bf16[32,32,256]{2,1,0:T(8,128)(2,1)} %copy.39), channel_id=1, source_target_pairs={{8,0},{16,8},{24,16},{32,24},{40,32},{48,40},{56,48},{64,56},{72,6... | collective-permute-start | bytes 1572872 | tf_op jit(solution)/shard_map/ppermute | solution.py:17
  51.0 4.1 copy-start.10
  53.1 2.0 copy-start.23
  55.1 2.6 copy-start
  59.3 4.1 copy-start.11
  59.3 4.1 copy-start.14
  83.5 2.2 copy-start.5
  87.7 2.2 copy-start.13
  91.1 5.5 copy-start.8
  92.9 2.1 copy-start.3
  101.2 2.6 copy-start.16
  104.3 1.8 copy-start.4
  104.3 2.6 copy-start.9
  104.3 3.3 copy-start.17
  132.2 1.9 copy-start.7
  133.8 79.9 %reduce-scatter.5.cloned.1.call-start = ((), (), s32[]{:S(2)}) async-start(), calls=%async_computation.3 | async-start | bytes 1179648 | tf_op jit(solution)/shard_map/reduce_scatter | solution.py:94
  134.1 2.3 copy-start.18
  155.4 24.6 %collective-permute-start.2 = (f32[32,32,256]{2,1,0:T(8,128)S(1)}, f32[32,32,256]{2,1,0:T(8,128)S(1)}, u32[]{:S(2)}, u32[]{:S(2)}) collective-permute-start(f32[32,32,256]{2,1,0:T(8,128)S(1)} %get-tuple-element.13), channel_id=1, source_target_pairs={{0,248},{8,0},{16,8},{24,16},{32,24},{40,32},{48,40},{56,48},{64,5... | collective-permute-start | bytes 3145736 | tf_op jit(solution)/shard_map/ppermute | solution.py:24
  157.2 27.6 %collective-permute-start.3 = (f32[32,32,256]{2,1,0:T(8,128)S(1)}, f32[32,32,256]{2,1,0:T(8,128)S(1)}, u32[]{:S(2)}, u32[]{:S(2)}) collective-permute-start(f32[32,32,256]{2,1,0:T(8,128)S(1)} %get-tuple-element.14), channel_id=1, source_target_pairs={{0,8},{8,16},{16,24},{24,32},{32,40},{40,48},{48,56},{56,64},{64,7... | collective-permute-start | bytes 3145736 | tf_op jit(solution)/shard_map/ppermute | solution.py:24
  185.1 29.5 %copy-start.20 = (f32[4,4096]{1,0:T(4,128)S(1)}, f32[4,4096]{1,0:T(4,128)}, u32[]{:S(2)}) copy-start(f32[4,4096]{1,0:T(4,128)} %param.20) | copy-start | bytes 196612
  185.2 29.5 %copy-start.21 = (s32[4096]{0:T(1024)S(1)}, s32[4096]{0:T(1024)}, u32[]{:S(2)}) copy-start(s32[4096]{0:T(1024)} %param.21) | copy-start | bytes 49156
  186.8 367.2 %all-reduce.3.cloned.1.call-start = ((), (), s32[]{:S(2)}) async-start(), calls=%async_computation.4 | async-start | bytes 262144
  (8 other events, 12.1 us)
Sparse Core Ops, SparseCore 0:
  134.0 29.4 reduce-scatter.2
  186.9 26.7 reduce-scatter.4
  308.2 245.7 all-reduce.2
where the time goes:
time: 564 us; the launch traced here: 562 us
  waiting for transfers between devices  297 us (53%)
  other arithmetic  149 us (26%)
  local copies, waits for them, and re-layouts  33.8 us (6%)
  blocking collectives  29.5 us (5%)
  matrix products  29.3 us (5%)
  between operations  14.2 us (3%)
  starting transfers between devices  8.78 us (2%)
    unnamed x4, waiting for transfers between devices  243 us
    scatter-add x1, other arithmetic, shards(): jax.ops.segment_sum(weighted.reshape(-1), panel_params.reshape(-1), num_s...  93.3 us
    ppermute x2, waiting for transfers between devices, shifted(): lax.ppermute(x, axis, [(i, (i + by) % devices) for i in range(devices)])  27.6 us
    reduce_scatter x1, waiting for transfers between devices, shards(): lax.psum_scatter(own_terms, 'sub', scatter_dimension=1, tiled=True)  26.8 us
    unnamed x59, local copies, waits for them, and re-layouts  16.3 us
    all_gather x1, blocking collectives, shards(): lax.all_gather(forward_rhs, 'sub', axis=1, tiled=True)  16.1 us
    scatter-add x1, other arithmetic, shards(): jax.ops.segment_sum(far_back, far_cols, num_segments=3 * clusters)  13.5 us
    scatter-add x1, other arithmetic, shards(): jax.ops.segment_sum(far_out, far_rows, num_segments=clusters)  13.5 us
  transfers between devices with their start and end apart: 7, of which 4 were waited for; matrix products, arithmetic and copies ran while one was open for 10% of the time, Pallas kernels for 0%

commit v1 on v0

v1 whole, which is shorter than its diff:
```python
import jax
import jax.numpy as jnp
from jax import lax
from jax.experimental import pallas as pl
from jax.experimental.pallas import tpu as pltpu
from jax.sharding import PartitionSpec as P

MESH = pl.DeviceIdType.MESH
F32 = jnp.float32
BF16 = jnp.bfloat16

GROUPS = 32
MEMBERS = 8
RING = 4
CG = 32
COLS = 4
CS = 128
RANK = 32
FAR = 128
NEAR = 32
STEPS = 8
WIDE = 4 * CG


def place():
    c = lax.axis_index("clus")
    s = lax.axis_index("sub")
    y = s // 2
    p = s % 2
    up, down, far = (y + 1) % RING, (y + 3) % RING, (y + 2) % RING
    return c, s, y, p, up, down, far


def meet(peers):
    barrier = pltpu.get_barrier_semaphore()
    for peer in peers:
        pl.semaphore_signal(barrier, inc=1, device_id=peer, device_id_type=MESH)
    pl.semaphore_wait(barrier, len(peers))


def gather_kernel(x_ref, w_ref, xo, wo, send, recv, local):
    c, s, y, p, up, down, far = place()
    to_up, to_down = {"sub": 2 * up + p}, {"sub": 2 * down + p}
    to_mate = {"sub": 2 * y + 1 - p}
    to_next, to_prev = {"clus": (c + 1) % GROUPS}, {"clus": (c + GROUPS - 1) % GROUPS}
    meet([to_up, to_down, to_mate, to_next, to_prev])

    def copy(src, dst, k, peer):
        return pltpu.make_async_remote_copy(
            src_ref=src, dst_ref=dst, send_sem=send.at[k], recv_sem=recv.at[k], device_id=peer, device_id_type=MESH
        )

    own = pl.ds(CG, CG)
    subs = [2 * t + p for t in (y, down, up, far)]
    mates = [2 * t + 1 - p for t in (y, down, up, far)]

    started = []

    def go(src, dst, k, peer):
        d = copy(src, dst, k, peer)
        d.start()
        started.append(d)

    def arrived(ref, k):
        copy(ref, ref, k, to_mate).wait_recv()

    keep_x = pltpu.make_async_copy(x_ref, xo.at[own, :, s], local.at[0])
    keep_w = pltpu.make_async_copy(w_ref, wo.at[:, :, s], local.at[1])
    go(w_ref, wo.at[:, :, s], 0, to_up)
    go(x_ref, xo.at[own, :, s], 4, to_down)
    go(w_ref, wo.at[:, :, s], 1, to_down)
    go(x_ref, xo.at[own, :, s], 3, to_up)
    go(x_ref, xo.at[pl.ds(0, CG), :, s], 6, to_next)
    go(x_ref, xo.at[pl.ds(2 * CG, CG), :, s], 10, to_prev)
    go(w_ref, wo.at[:, :, s], 14, to_mate)
    go(x_ref, xo.at[own, :, s], 18, to_mate)
    keep_x.start()
    keep_w.start()

    def got_w(i):
        ref = wo.at[:, :, subs[i]]
        arrived(ref, i - 1)
        if i == 2:
            go(ref, ref, 2, to_down)
        go(ref, ref, 14 + i, to_mate)

    def got_x(i):
        ref = xo.at[own, :, subs[i]]
        arrived(ref, 2 + i)
        if i == 1:
            go(ref, ref, 5, to_up)
        go(ref, xo.at[pl.ds(0, CG), :, subs[i]], 6 + i, to_next)
        go(ref, xo.at[pl.ds(2 * CG, CG), :, subs[i]], 10 + i, to_prev)
        go(ref, ref, 18 + i, to_mate)

    def got_side(i):
        left = xo.at[pl.ds(0, CG), :, subs[i]]
        arrived(left, 6 + i)
        go(left, left, 22 + i, to_mate)
        right = xo.at[pl.ds(2 * CG, CG), :, subs[i]]
        arrived(right, 10 + i)
        go(right, right, 26 + i, to_mate)

    got_x(1)
    got_w(2)
    got_x(2)
    got_w(1)
    got_side(0)
    got_x(3)
    got_w(3)
    got_side(1)
    got_side(2)
    got_side(3)
    for i in range(4):
        arrived(wo.at[:, :, mates[i]], 14 + i)
        arrived(xo.at[own, :, mates[i]], 18 + i)
        arrived(xo.at[pl.ds(0, CG), :, mates[i]], 22 + i)
        arrived(xo.at[pl.ds(2 * CG, CG), :, mates[i]], 26 + i)
    for d in started:
        d.wait_send()
    keep_x.wait()
    keep_w.wait()


def real_form(ref, b, sign):
    re, im = ref[b, 0], ref[b, 1]
    if sign > 0:
        top, low = [re, im], [-im, re]
    else:
        top, low = [re, -im], [im, re]
    return jnp.concatenate([jnp.concatenate(top, axis=1), jnp.concatenate(low, axis=1)], axis=0)


NT = (((1,), (1,)), ((), ()))
NN = (((1,), (0,)), ((), ()))


def mm(a, b, dims):
    return lax.dot_general(a, b, dims, preferred_element_type=F32)


def block_kernel(far_ids, ranks, near_ids, x_ref, w_ref, u_ref, v_ref, n_ref, out, acc):
    step = pl.program_id(0)
    first = lax.axis_index("clus") * CG
    total = GROUPS * CG

    @pl.when(step == 0)
    def _():
        acc[...] = jnp.zeros_like(acc)

    def row_of(ids, b):
        return jnp.clip(ids[0, b] - first, 0, CG - 1)

    def col_of(ids, b):
        return jnp.clip((ids[1, b] - first + CG + total) % total, 0, 3 * CG - 1)

    def slot_of(col):
        return jnp.where(col < CG, col, jnp.where(col < 2 * CG, col + CG, col - CG))

    def rows(ref, r, conj):
        re, im = ref[r, 0], ref[r, 1]
        return jnp.concatenate([re, -im if conj else im], axis=1)

    lane = lax.broadcasted_iota(jnp.int32, (1, 256), 1)
    per = FAR // STEPS
    for g in range(per // 4):
        local = [4 * g + i for i in range(4)]
        slots = [step * per + b for b in local]
        r = [row_of(far_ids, b) for b in slots]
        col = [col_of(far_ids, b) for b in slots]
        keep = [((lane // 64 == i) & (lane % RANK < ranks[slots[i]])).astype(F32) for i in range(4)]
        vm = jnp.concatenate([real_form(v_ref, b, -1) for b in local], axis=0)
        um = jnp.concatenate([real_form(u_ref, b, 1) for b in local], axis=0)

        def masked(m):
            parts = [(m[32 * i : 32 * i + 32] * keep[i]).astype(BF16) for i in range(4)]
            return jnp.concatenate(parts, axis=0)

        x4 = jnp.concatenate([rows(x_ref, k, False) for k in col], axis=0)
        w4 = jnp.concatenate([rows(w_ref, k, True) for k in r], axis=0)
        fwd = mm(masked(mm(x4, vm, NT)), um, NN)
        adj = mm(masked(mm(w4, um, NT)), vm, NN)
        for i in range(4):
            acc[3 * CG + r[i]] += fwd[32 * i : 32 * i + 32]
            acc[slot_of(col[i])] += adj[32 * i : 32 * i + 32]
    per = NEAR // STEPS
    for b in range(per):
        slot = step * per + b
        r, col = row_of(near_ids, slot), col_of(near_ids, slot)
        nm = real_form(n_ref, b, -1)
        acc[3 * CG + r] += mm(rows(x_ref, col, False), nm, NT)
        acc[slot_of(col)] += mm(rows(w_ref, r, True), nm, NN)

    @pl.when(step == STEPS - 1)
    def _():
        def one(k, carry):
            a = acc[k]
            out[k, 0] = a[:, :CS].astype(BF16)
            out[k, 1] = a[:, CS:].astype(BF16)
            return carry

        lax.fori_loop(0, WIDE, one, 0)


HALF = 2 * CG


def scatter_kernel(part, fwd, adj, sens, mate_in, mine, pass_in, done_in, side_out, side_in, send, recv):
    c, s, y, p, up, down, far = place()
    to_up, to_down = {"sub": 2 * up + p}, {"sub": 2 * down + p}
    to_mate = {"sub": 2 * y + 1 - p}
    to_next, to_prev = {"clus": (c + 1) % GROUPS}, {"clus": (c + GROUPS - 1) % GROUPS}
    meet([to_up, to_down, to_mate, to_next, to_prev])
    started = []

    def copy(src, dst, k, peer):
        return pltpu.make_async_remote_copy(
            src_ref=src, dst_ref=dst, send_sem=send.at[k], recv_sem=recv.at[k], device_id=peer, device_id_type=MESH
        )

    def go(src, dst, k, peer):
        d = copy(src, dst, k, peer)
        d.start()
        started.append(d)

    def arrived(ref, k):
        copy(ref, ref, k, to_mate).wait_recv()

    tos = [far, up, down, y]
    for ph in range(2):
        for j in range(4):
            go(part.at[pl.ds(ph * HALF, HALF), :, 2 * tos[j] + 1 - p], mate_in.at[ph, j], 4 * ph + j, to_mate)

    chunk = 8

    def pair_sum(ph, j, lo, hi, extra=None):
        who = 2 * tos[j] + p

        def one(i, carry):
            at = pl.ds(lo + i * chunk, chunk)
            a = part[pl.ds(ph * HALF + lo + i * chunk, chunk), :, who].astype(F32) + mate_in[ph, j, at].astype(F32)
            if extra is not None:
                a = a + extra[pl.ds(i * chunk, chunk)].astype(F32)
            mine[ph, j, at] = a.astype(BF16)
            return carry

        lax.fori_loop(0, (hi - lo) // chunk, one, 0)

    A, B = pl.ds(0, CG), pl.ds(CG, CG)
    for ph in range(2):
        base = 8 + 6 * ph
        arrived(mate_in.at[ph, 0], 4 * ph)
        pair_sum(ph, 0, 0, CG)
        go(mine.at[ph, 0, A], pass_in.at[ph, 0], base, to_up)
        pair_sum(ph, 0, CG, HALF)
        go(mine.at[ph, 0, B], pass_in.at[ph, 1], base + 1, to_down)
        arrived(mate_in.at[ph, 1], 4 * ph + 1)
        pair_sum(ph, 1, CG, HALF)
        go(mine.at[ph, 1, B], done_in.at[ph, 0, B], base + 2, to_up)
        arrived(mate_in.at[ph, 2], 4 * ph + 2)
        pair_sum(ph, 2, 0, CG)
        go(mine.at[ph, 2, A], done_in.at[ph, 1, A], base + 3, to_down)
        arrived(pass_in.at[ph, 0], base)
        pair_sum(ph, 1, 0, CG, pass_in.at[ph, 0])
        go(mine.at[ph, 1, A], done_in.at[ph, 0, A], base + 4, to_up)
        arrived(pass_in.at[ph, 1], base + 1)
        pair_sum(ph, 2, CG, HALF, pass_in.at[ph, 1])
        go(mine.at[ph, 2, B], done_in.at[ph, 1, B], base + 5, to_down)

    def finish(ph):
        base = 8 + 6 * ph
        arrived(mate_in.at[ph, 3], 4 * ph + 3)
        arrived(done_in.at[ph, 0, B], base + 2)
        arrived(done_in.at[ph, 1, A], base + 3)
        arrived(done_in.at[ph, 0, A], base + 4)
        arrived(done_in.at[ph, 1, B], base + 5)

    def whole(ph, at, n):
        a = part[pl.ds(ph * HALF + at, n), :, s].astype(F32) + mate_in[ph, 3, pl.ds(at, n)].astype(F32)
        return a + done_in[ph, 0, pl.ds(at, n)].astype(F32) + done_in[ph, 1, pl.ds(at, n)].astype(F32)

    finish(0)

    def edge(i, carry):
        at = i * chunk
        side_out[pl.ds(at, chunk)] = whole(0, at, chunk)
        return carry

    lax.fori_loop(0, CG // chunk, edge, 0)
    go(side_out.at[A], side_in.at[0], 20, to_prev)
    lax.fori_loop(CG // chunk, HALF // chunk, edge, 0)
    go(side_out.at[B], side_in.at[1], 21, to_next)
    finish(1)
    arrived(side_in.at[0], 20)
    arrived(side_in.at[1], 21)

    def last(i, carry):
        at = i * chunk
        here = pl.ds(at, chunk)
        a = whole(1, at, chunk) + side_in[0, here] + side_in[1, here]
        f = whole(1, CG + at, chunk)
        fwd[here] = f
        adj[here, 0] = a[:, 0]
        adj[here, 1] = -a[:, 1]
        prod = f * a
        sens[here] = jnp.sum(prod[:, 0] + prod[:, 1], axis=1) * (1.0 / (MEMBERS * COLS))
        return carry

    lax.fori_loop(0, CG // chunk, last, 0)
    for d in started:
        d.wait_send()


def param_kernel(sens, params, weights, counts, out, grid, got, row, ring, send, recv, send2, recv2):
    c, s, y, p, up, down, far = place()
    barrier = pltpu.get_barrier_semaphore()
    for off in range(1, MEMBERS):
        pl.semaphore_signal(barrier, inc=1, device_id={"sub": (s + off) % MEMBERS}, device_id_type=MESH)

    def tell(off, carry):
        pl.semaphore_signal(barrier, inc=1, device_id={"clus": (c + off) % GROUPS}, device_id_type=MESH)
        return carry

    lax.fori_loop(1, GROUPS, tell, 0)

    devices = GROUPS * MEMBERS
    high = lax.broadcasted_iota(jnp.int32, (devices, CS), 0)
    low = lax.broadcasted_iota(jnp.int32, (CS, CS), 0)
    one, zero = jnp.ones((), F32), jnp.zeros((), F32)

    def cluster(k, total):
        at = pl.multiple_of(k * CS, CS)
        value = sens[pl.ds(k, 1), :]
        count = counts[pl.ds(k, 1), :]
        left, right = [], []
        for m in range(4):
            q = params[pl.ds(m, 1), pl.ds(at, CS)]
            wt = weights[pl.ds(m, 1), pl.ds(at, CS)]
            val = jnp.where(count > m, wt * value, zero)
            top = val.astype(BF16).astype(F32)
            rest = val - top
            owner = q // CS
            owner = (owner % MEMBERS) * GROUPS + owner // MEMBERS
            left.append(jnp.where(high == owner, one, zero).astype(BF16))
            hit = low == q % CS
            right.append(
                jnp.concatenate(
                    [jnp.where(hit, top, zero).astype(BF16), jnp.where(hit, rest, zero).astype(BF16)], axis=0
                )
            )
        g = mm(jnp.concatenate(left, axis=1), jnp.concatenate(right, axis=1), NT)
        return total + (g[:, :CS] + g[:, CS:])

    grid[...] = lax.fori_loop(0, CG, cluster, jnp.zeros((devices, CS), F32))
    pl.semaphore_wait(barrier, MEMBERS - 1 + GROUPS - 1)

    def part_of(member):
        return grid.at[pl.ds(pl.multiple_of(member * GROUPS, GROUPS), GROUPS)]

    sent = []
    for off in range(1, MEMBERS):
        to = (s + off) % MEMBERS
        d = pltpu.make_async_remote_copy(
            src_ref=part_of(to), dst_ref=got.at[off - 1], send_sem=send.at[off - 1], recv_sem=recv.at[off - 1],
            device_id={"sub": to}, device_id_type=MESH,
        )
        d.start()
        sent.append(d)
    total = grid[pl.ds(pl.multiple_of(s * GROUPS, GROUPS), GROUPS), :]
    for d in sent:
        d.wait_recv()
    for off in range(MEMBERS - 1):
        total = total + got[off]
    for k in range(GROUPS):
        row[k] = total[k : k + 1]

    def copy(off):
        return pltpu.make_async_remote_copy(
            src_ref=row.at[(c + off) % GROUPS], dst_ref=ring.at[off - 1], send_sem=send2.at[off - 1],
            recv_sem=recv2.at[off - 1], device_id={"clus": (c + off) % GROUPS}, device_id_type=MESH,
        )

    def start(off, carry):
        copy(off).start()
        return carry

    def wait(off, carry):
        copy(off).wait()
        return carry

    lax.fori_loop(1, GROUPS, start, 0)
    for d in sent:
        d.wait_send()
    lax.fori_loop(1, GROUPS, wait, 0)
    final = row[c]
    for k in range(GROUPS - 1):
        final = final + ring[k]
    out[...] = final


ANY = pl.BlockSpec(memory_space=pl.ANY)
VMEM = pl.BlockSpec(memory_space=pltpu.VMEM)


def split_form(x):
    n = x.shape[0]
    return x.reshape(n, COLS, 2, CS).transpose(0, 2, 1, 3)


def joined(x):
    n = x.shape[0]
    return x.transpose(0, 2, 1, 3).reshape(n, COLS, 2 * CS)


def shards(x, w, far_ids, ranks, far_left, far_right, near_ids, near, params, weights, counts):
    wide_x, wide_w = pl.pallas_call(
        gather_kernel,
        out_shape=(
            jax.ShapeDtypeStruct((3 * CG, 2, MEMBERS, COLS, CS), BF16),
            jax.ShapeDtypeStruct((CG, 2, MEMBERS, COLS, CS), BF16),
        ),
        in_specs=[VMEM, VMEM],
        out_specs=(ANY, ANY),
        scratch_shapes=[
            pltpu.SemaphoreType.DMA((30,)),
            pltpu.SemaphoreType.DMA((30,)),
            pltpu.SemaphoreType.DMA((2,)),
        ],
        compiler_params=pltpu.CompilerParams(collective_id=0, has_side_effects=True),
        name="gather",
    )(split_form(x), split_form(w))
    wide_x = wide_x.reshape(3 * CG, 2, MEMBERS * COLS, CS)
    wide_w = wide_w.reshape(CG, 2, MEMBERS * COLS, CS)

    per, pern = FAR // STEPS, NEAR // STEPS
    part = pl.pallas_call(
        block_kernel,
        out_shape=jax.ShapeDtypeStruct((WIDE, 2, MEMBERS * COLS, CS), BF16),
        grid_spec=pltpu.PrefetchScalarGridSpec(
            num_scalar_prefetch=3,
            grid=(STEPS,),
            in_specs=[
                VMEM,
                VMEM,
                pl.BlockSpec((per, 2, RANK, CS), lambda i, *_: (i, 0, 0, 0)),
                pl.BlockSpec((per, 2, RANK, CS), lambda i, *_: (i, 0, 0, 0)),
                pl.BlockSpec((pern, 2, CS, CS), lambda i, *_: (i, 0, 0, 0)),
            ],
            out_specs=VMEM,
            scratch_shapes=[pltpu.VMEM((WIDE, MEMBERS * COLS, 2 * CS), F32)],
        ),
        compiler_params=pltpu.CompilerParams(vmem_limit_bytes=40 << 20),
        name="blocks",
    )(far_ids, ranks, near_ids, wide_x, wide_w, far_left, far_right, near)
    part = part.reshape(WIDE, 2, MEMBERS, COLS, CS)

    fwd, adj, sens = pl.pallas_call(
        scatter_kernel,
        out_shape=(
            jax.ShapeDtypeStruct((CG, 2, COLS, CS), F32),
            jax.ShapeDtypeStruct((CG, 2, COLS, CS), F32),
            jax.ShapeDtypeStruct((CG, CS), F32),
        ),
        in_specs=[VMEM],
        out_specs=(VMEM, VMEM, VMEM),
        scratch_shapes=[
            pltpu.VMEM((2, 4, HALF, 2, COLS, CS), BF16),
            pltpu.VMEM((2, 3, HALF, 2, COLS, CS), BF16),
            pltpu.VMEM((2, 2, CG, 2, COLS, CS), BF16),
            pltpu.VMEM((2, 2, HALF, 2, COLS, CS), BF16),
            pltpu.VMEM((HALF, 2, COLS, CS), F32),
            pltpu.VMEM((2, CG, 2, COLS, CS), F32),
            pltpu.SemaphoreType.DMA((22,)),
            pltpu.SemaphoreType.DMA((22,)),
        ],
        compiler_params=pltpu.CompilerParams(collective_id=1, has_side_effects=True, vmem_limit_bytes=40 << 20),
        name="scatter",
    )(part)

    grad = pl.pallas_call(
        param_kernel,
        out_shape=jax.ShapeDtypeStruct((1, CS), F32),
        in_specs=[VMEM] * 4,
        out_specs=VMEM,
        scratch_shapes=[
            pltpu.VMEM((GROUPS * MEMBERS, CS), F32),
            pltpu.VMEM((MEMBERS - 1, GROUPS, CS), F32),
            pltpu.VMEM((GROUPS, 1, CS), F32),
            pltpu.VMEM((GROUPS - 1, 1, CS), F32),
            pltpu.SemaphoreType.DMA((MEMBERS - 1,)),
            pltpu.SemaphoreType.DMA((MEMBERS - 1,)),
            pltpu.SemaphoreType.DMA((GROUPS - 1,)),
            pltpu.SemaphoreType.DMA((GROUPS - 1,)),
        ],
        compiler_params=pltpu.CompilerParams(collective_id=2, has_side_effects=True),
        name="params",
    )(sens, params, weights, counts.reshape(CG, CS))
    return joined(fwd), joined(adj), grad.reshape(CS)


def solution(mesh):
    rhs = P("clus", "sub", None)
    blocks = P(("clus", "sub"), None, None, None)
    both = ("clus", "sub")
    in_specs = (rhs, rhs, P(None, both), P(both), blocks, blocks, P(None, both), blocks)
    in_specs += (P(None, "clus"), P(None, "clus"), P("clus"))
    out_specs = (rhs, rhs, P(both))
    return jax.shard_map(shards, mesh=mesh, in_specs=in_specs, out_specs=out_specs, check_vma=False)
```

time: 564 us -> 97 us (0.17)
  waiting for transfers between devices: 297 us -> 0 us
  other arithmetic: 149 us -> 0 us
  Pallas kernels: 0 us -> 83.7 us
  blocking collectives: 29.5 us -> 0 us
  matrix products: 29.3 us -> 0 us
  local copies, waits for them, and re-layouts: 33.8 us -> 12.3 us
  between operations: 14.2 us -> 0.69 us
  starting transfers between devices: 8.78 us -> 0 us
    unnamed x4 -> x0, waiting for transfers between devices: 243 us -> none
    scatter-add x5 -> x0, other arithmetic: 130 us -> none  [the longest x1 93.3 us: shards(): jax.ops.segment_sum(weighted.reshape(-1), panel_params.reshape(-1), num_s...]
    pallas_call x0 -> x4, Pallas kernels: none -> 83.7 us  [the longest x1 25.8 us: shards(): pl.pallas_call(gather_kernel, out_shape=(jax.ShapeDtypeStruct((3 * CG, 2,...]
    all_gather x2 -> x0, blocking collectives: 29.5 us -> none  [the longest x1 16.1 us: shards(): lax.all_gather(forward_rhs, 'sub', axis=1, tiled=True)]
    dot_general x24 -> x0, matrix products: 29.3 us -> none  [the longest x6 8.23 us: complex_mix(): jnp.einsum(einsum_form, imag_lhs, imag_rhs, preferred_element_type=jnp.fl...]
    ppermute x4 -> x0, waiting for transfers between devices: 27.6 us -> none  [the longest x2 27.6 us: shifted(): lax.ppermute(x, axis, [(i, (i + by) % devices) for i in range(devices)])]
    reduce_scatter x2 -> x0, waiting for transfers between devices: 26.8 us -> none  [the longest x1 26.8 us: shards(): lax.psum_scatter(own_terms, 'sub', scatter_dimension=1, tiled=True)]
    ppermute x4 -> x0, starting transfers between devices: 8.44 us -> none  [the longest x1 6.14 us: extended(): after = lax.ppermute(leading, axis, down)]
  transfers between devices with their start and end apart: 7 -> 0, of which waited for: 4 -> 0; matrix products, arithmetic and copies ran while one was open for 10% -> 0% of each run, Pallas kernels for 0% -> 0%
where the time goes in v1:
time: 97 us; the launch traced here: 96.6 us
  Pallas kernels  83.7 us (86%)
  local copies, waits for them, and re-layouts  12.3 us (13%)
    pallas_call x1, Pallas kernels, shards(): pl.pallas_call(gather_kernel, out_shape=(jax.ShapeDtypeStruct((3 * CG, 2,...  25.8 us
    pallas_call x1, Pallas kernels, shards(): pl.pallas_call(param_kernel, out_shape=jax.ShapeDtypeStruct((1, CS), F32)...  24.3 us
    pallas_call x1, Pallas kernels, shards(): pl.pallas_call(scatter_kernel, out_shape=(jax.ShapeDtypeStruct((CG, 2, CO...  17 us
    pallas_call x1, Pallas kernels, shards(): pl.pallas_call(block_kernel, out_shape=jax.ShapeDtypeStruct((WIDE, 2, MEM...  16.6 us
    unnamed x21, local copies, waits for them, and re-layouts  12.3 us

profile of v1, /device:TPU:1, one launch (start us, length us, event | category | flops | bytes accessed | tf_op | source)
XLA Modules:
  0.0 96.6 jit_solution(6550770588128535277)
XLA Ops:
  0.6 25.8 %gather.1 = (bf16[96,2,8,4,128]{4,3,2,1,0:T(4,128)(2,1)}, bf16[32,2,8,4,128]{4,3,2,1,0:T(4,128)(2,1)}) custom-call(bf16[32,2,4,128]{3,2,1,0:T(4,128)(2,1)} %bitcast.22, bf16[32,2,4,128]{3,2,1,0:T(4,128)(2,1)} %bitcast.23), custom_call_target="tpu_custom_call" | custom-call | tf_op jit(solution)/shard_map/gather/pallas_call | solution.py:416
  26.4 0.0 copy-start
  26.5 1.6 %copy-done = bf16[128,2,32,128]{3,2,1,0:T(8,128)(2,1)S(1)} copy-done((bf16[128,2,32,128]{3,2,1,0:T(8,128)(2,1)S(1)}, bf16[128,2,32,128]{3,2,1,0:T(8,128)(2,1)}, u32[]{:S(2)}) %copy-start) | copy-done | bytes 2097176
  28.0 0.0 copy-start.1
  28.0 1.6 %copy-done.1 = bf16[128,2,32,128]{3,2,1,0:T(8,128)(2,1)S(1)} copy-done((bf16[128,2,32,128]{3,2,1,0:T(8,128)(2,1)S(1)}, bf16[128,2,32,128]{3,2,1,0:T(8,128)(2,1)}, u32[]{:S(2)}) %copy-start.1) | copy-done | bytes 2097176
  29.6 0.0 copy-start.2
  29.6 1.6 %copy-done.2 = bf16[32,2,128,128]{3,2,1,0:T(8,128)(2,1)S(1)} copy-done((bf16[32,2,128,128]{3,2,1,0:T(8,128)(2,1)S(1)}, bf16[32,2,128,128]{3,2,1,0:T(8,128)(2,1)}, u32[]{:S(2)}) %copy-start.2) | copy-done | bytes 2097176
  31.2 0.0 copy-start.3
  31.2 1.4 %copy-done.3 = bf16[96,2,8,4,128]{4,3,2,1,0:T(4,128)(2,1)S(1)} copy-done((bf16[96,2,8,4,128]{4,3,2,1,0:T(4,128)(2,1)S(1)}, bf16[96,2,8,4,128]{4,3,2,1,0:T(4,128)(2,1)}, u32[]{:S(2)}) %copy-start.3) | copy-done | bytes 1572888
  32.6 0.0 copy-start.4
  32.6 1.0 %copy-done.4 = bf16[32,2,8,4,128]{4,3,2,1,0:T(4,128)(2,1)S(1)} copy-done((bf16[32,2,8,4,128]{4,3,2,1,0:T(4,128)(2,1)S(1)}, bf16[32,2,8,4,128]{4,3,2,1,0:T(4,128)(2,1)}, u32[]{:S(2)}) %copy-start.4) | copy-done | bytes 524312
  33.7 0.7 copy-done.6
  34.3 0.0 copy-start.7
  34.4 0.7 copy-done.7
  35.0 0.0 copy-start.8
  35.0 0.7 copy-done.8
  35.7 16.6 %blocks.1 = bf16[128,2,32,128]{3,2,1,0:T(8,128)(2,1)S(1)} custom-call(s32[2,128]{1,0:T(2,128)S(1)} %copy-done.6, s32[128]{0:T(128)S(1)} %copy-done.8, s32[2,32]{1,0:T(2,128)S(1)} %copy-done.7, bf16[96,2,32,128]{3,2,1,0:T(8,128)(2,1)S(1)} %bitcast.18, bf16[32,2,32,128]{3,2,1,0:T(8,128)(2,1)S(1)} %bitcast.19, bf16[128,2,32,128]{3,2,1,0:T(8,128)(2,1)S(1)} %copy-done, ...), custom_call_target="tpu_custom_call" | custom-call | tf_op jit(solution)/shard_map/blocks/pallas_call | solution.py:436
  52.3 17.0 %scatter.1 = (f32[32,2,4,128]{3,2,1,0:T(4,128)S(1)}, f32[32,2,4,128]{3,2,1,0:T(4,128)S(1)}, f32[32,128]{1,0:T(8,128)S(1)}) custom-call(bf16[128,2,8,4,128]{4,3,2,1,0:T(4,128)(2,1)S(1)} %bitcast.17), custom_call_target="tpu_custom_call" | custom-call | tf_op jit(solution)/shard_map/scatter/pallas_call | solution.py:457
  69.3 0.0 copy-start.5
  69.3 0.6 copy-done.5
  69.9 24.3 %params.2 = f32[1,128]{1,0:T(1,128)} custom-call(f32[32,128]{1,0:T(8,128)} %copy-done.5, s32[4,4096]{1,0:T(4,128)} %params.3, f32[4,4096]{1,0:T(4,128)} %weights.1, s32[32,128]{1,0:T(8,128)} %bitcast.24), custom_call_target="tpu_custom_call" | custom-call | tf_op jit(solution)/shard_map/params/pallas_call | solution.py:480
  94.2 0.7 copy.17
  94.8 0.7 copy.18
  95.5 1.1 %copy.19 = f32[128]{0:T(128)} copy(f32[128]{0:T(128)} %bitcast.25) | data formatting | bytes 1024
  (1 shorter events, 0.0 us)
Async XLA Ops:
  26.4 1.6 %copy-start = (bf16[128,2,32,128]{3,2,1,0:T(8,128)(2,1)S(1)}, bf16[128,2,32,128]{3,2,1,0:T(8,128)(2,1)}, u32[]{:S(2)}) copy-start(bf16[128,2,32,128]{3,2,1,0:T(8,128)(2,1)} %u_ref.1) | copy-start | bytes 6291460
  28.0 1.6 %copy-start.1 = (bf16[128,2,32,128]{3,2,1,0:T(8,128)(2,1)S(1)}, bf16[128,2,32,128]{3,2,1,0:T(8,128)(2,1)}, u32[]{:S(2)}) copy-start(bf16[128,2,32,128]{3,2,1,0:T(8,128)(2,1)} %v_ref.1) | copy-start | bytes 6291460
  29.6 1.6 %copy-start.2 = (bf16[32,2,128,128]{3,2,1,0:T(8,128)(2,1)S(1)}, bf16[32,2,128,128]{3,2,1,0:T(8,128)(2,1)}, u32[]{:S(2)}) copy-start(bf16[32,2,128,128]{3,2,1,0:T(8,128)(2,1)} %n_ref.1) | copy-start | bytes 6291460
  31.2 1.4 %copy-start.3 = (bf16[96,2,8,4,128]{4,3,2,1,0:T(4,128)(2,1)S(1)}, bf16[96,2,8,4,128]{4,3,2,1,0:T(4,128)(2,1)}, u32[]{:S(2)}) copy-start(bf16[96,2,8,4,128]{4,3,2,1,0:T(4,128)(2,1)} %get-tuple-element.8) | copy-start | bytes 4718596
  32.6 1.0 %copy-start.4 = (bf16[32,2,8,4,128]{4,3,2,1,0:T(4,128)(2,1)S(1)}, bf16[32,2,8,4,128]{4,3,2,1,0:T(4,128)(2,1)}, u32[]{:S(2)}) copy-start(bf16[32,2,8,4,128]{4,3,2,1,0:T(4,128)(2,1)} %get-tuple-element.9) | copy-start | bytes 1572868
  33.7 0.7 copy-start.6
  34.3 0.7 copy-start.7
  35.0 0.7 copy-start.8
  69.3 0.6 copy-start.5

commit v2 on v0

v2 whole, which is shorter than its diff:
```python
import jax
import jax.numpy as jnp
from jax import lax
from jax.experimental import pallas as pl
from jax.experimental.pallas import tpu as pltpu
from jax.sharding import PartitionSpec as P

MESH = pl.DeviceIdType.MESH
F32 = jnp.float32
BF16 = jnp.bfloat16

GROUPS = 32
MEMBERS = 8
RING = 4
CG = 32
COLS = 4
CS = 128
RANK = 32
FAR = 128
NEAR = 32
SEGS = 4
WIDE = 4 * CG


def place():
    c = lax.axis_index("clus")
    s = lax.axis_index("sub")
    y = s // 2
    p = s % 2
    up, down, far = (y + 1) % RING, (y + 3) % RING, (y + 2) % RING
    return c, s, y, p, up, down, far


NT = (((1,), (1,)), ((), ()))
NN = (((1,), (0,)), ((), ()))


def mm(a, b, dims):
    return lax.dot_general(a, b, dims, preferred_element_type=F32)


def real_form(ref, b, sign):
    re, im = ref[b, 0], ref[b, 1]
    if sign > 0:
        top, low = [re, im], [-im, re]
    else:
        top, low = [re, -im], [im, re]
    return jnp.concatenate([jnp.concatenate(top, axis=1), jnp.concatenate(low, axis=1)], axis=0)


def rows(ref, r, conj):
    re, im = ref[r, 0], ref[r, 1]
    return jnp.concatenate([re, -im if conj else im], axis=1)


PHASES = ((0, 2 * CG), (2 * CG, CG), (3 * CG, CG))


def kernel(
    x_ref, w_ref, u_hbm, v_hbm, n_hbm, far_ids, ranks, near_ids, params, weights, counts,
    fwd, adj, grad,
    xo, wo, u_ref, v_ref, n_ref, ids, table, lists, prod, nprod, part, mate_in, mine, pass_in, done_in,
    side_out, side_in, sens, high_hot, low_hot, grid, got, row, ring,
    local, gsend, grecv, send, recv, psend, precv, csend, crecv,
):
    c, s, y, p, up, down, far = place()
    to_up, to_down = {"sub": 2 * up + p}, {"sub": 2 * down + p}
    to_mate = {"sub": 2 * y + 1 - p}
    to_next, to_prev = {"clus": (c + 1) % GROUPS}, {"clus": (c + GROUPS - 1) % GROUPS}
    barrier = pltpu.get_barrier_semaphore()

    def tell_sub(off, carry):
        pl.semaphore_signal(barrier, inc=1, device_id={"sub": (s + off) % MEMBERS}, device_id_type=MESH)
        return carry

    def tell_clus(off, carry):
        pl.semaphore_signal(barrier, inc=1, device_id={"clus": (c + off) % GROUPS}, device_id_type=MESH)
        return carry

    lax.fori_loop(1, MEMBERS, tell_sub, 0)
    lax.fori_loop(1, GROUPS, tell_clus, 0)

    own = pl.ds(CG, CG)
    keep = [
        pltpu.make_async_copy(w_ref, wo.at[:, :, s], local.at[0]),
        pltpu.make_async_copy(x_ref, xo.at[own, :, s], local.at[1]),
        pltpu.make_async_copy(u_hbm, u_ref, local.at[2]),
        pltpu.make_async_copy(v_hbm, v_ref, local.at[3]),
        pltpu.make_async_copy(n_hbm, n_ref, local.at[4]),
    ]
    for d in keep:
        d.start()

    first = c * CG
    total = GROUPS * CG
    big = 127
    ids[...] = jnp.full_like(ids, -1)
    ids[0:2, :] = far_ids[...]
    ids[2:4, 0:NEAR] = near_ids[...]
    sub_i = lax.broadcasted_iota(jnp.int32, (FAR, FAR), 0)
    lane_i = lax.broadcasted_iota(jnp.int32, (FAR, FAR), 1)
    slot_row = lax.broadcasted_iota(jnp.int32, (1, FAR), 1)
    table[...] = jnp.zeros_like(table)

    def order(key, payload, at, end_at):
        k = jnp.broadcast_to(key, (FAR, FAR))
        kt = k.T
        tie = (k == kt) & (lane_i < sub_i)
        ones = jnp.ones_like(k)
        zeros = jnp.zeros_like(k)
        rank = jnp.sum(jnp.where((k < kt) | tie, ones, zeros), axis=1, keepdims=True)
        opens = jnp.sum(jnp.where(tie, ones, zeros), axis=1, keepdims=True) == 0
        pay = jnp.broadcast_to(payload, (FAR, FAR)).T + jnp.where(opens, 1 << 20, 0)
        table[pl.ds(at, 1), :] = jnp.sum(jnp.where(rank == lane_i, pay, zeros), axis=0, keepdims=True)
        upto = jnp.sum(jnp.where(kt <= lane_i, ones, zeros), axis=0, keepdims=True)
        below = jnp.sum(jnp.where(kt < lane_i, ones, zeros), axis=0, keepdims=True)
        table[pl.ds(end_at, 1), :] = jnp.where(upto > below, upto, 0)

    for i, count in ((0, FAR), (1, NEAR)):
        live = slot_row < count
        r = jnp.clip(ids[2 * i : 2 * i + 1, :] - first, 0, CG - 1)
        q = jnp.clip((ids[2 * i + 1 : 2 * i + 2, :] - first + CG + total) % total, 0, 3 * CG - 1)
        payload = slot_row + q * 128 + r * 16384
        order(jnp.where(live, q, big), payload, 2 * i, 5 + 2 * i)
        order(jnp.where(live, r, big), payload, 2 * i + 1, 6 + 2 * i)
    table[4:5, :] = ranks[...]
    to_lists = pltpu.make_async_copy(table, lists, local.at[5])
    to_lists.start()

    pl.semaphore_wait(barrier, MEMBERS - 1 + GROUPS - 1)

    subs = [2 * t + p for t in (y, down, up, far)]
    mates = [2 * t + 1 - p for t in (y, down, up, far)]
    started = []

    def gcopy(src, dst, k, peer):
        return pltpu.make_async_remote_copy(
            src_ref=src, dst_ref=dst, send_sem=gsend.at[k], recv_sem=grecv.at[k], device_id=peer, device_id_type=MESH
        )

    def ggo(src, dst, k, peer):
        d = gcopy(src, dst, k, peer)
        d.start()
        started.append(d)

    def garrived(ref, k):
        gcopy(ref, ref, k, to_mate).wait_recv()

    left_x, right_x = pl.ds(0, CG), pl.ds(2 * CG, CG)
    ggo(w_ref, wo.at[:, :, s], 0, to_up)
    ggo(w_ref, wo.at[:, :, s], 1, to_down)
    ggo(w_ref, wo.at[:, :, s], 14, to_mate)
    ggo(x_ref, xo.at[left_x, :, s], 6, to_next)
    ggo(x_ref, xo.at[right_x, :, s], 10, to_prev)
    ggo(x_ref, xo.at[own, :, s], 3, to_up)
    ggo(x_ref, xo.at[own, :, s], 4, to_down)
    ggo(x_ref, xo.at[own, :, s], 18, to_mate)

    def got_w(i):
        ref = wo.at[:, :, subs[i]]
        garrived(ref, i - 1)
        if i == 2:
            ggo(ref, ref, 2, to_down)
        ggo(ref, ref, 14 + i, to_mate)

    def got_x(i):
        ref = xo.at[own, :, subs[i]]
        garrived(ref, 2 + i)
        if i == 1:
            ggo(ref, ref, 5, to_up)
        ggo(ref, xo.at[left_x, :, subs[i]], 6 + i, to_next)
        ggo(ref, xo.at[right_x, :, subs[i]], 10 + i, to_prev)
        ggo(ref, ref, 18 + i, to_mate)

    def got_side(i):
        left = xo.at[left_x, :, subs[i]]
        garrived(left, 6 + i)
        ggo(left, left, 22 + i, to_mate)
        right = xo.at[right_x, :, subs[i]]
        garrived(right, 10 + i)
        ggo(right, right, 26 + i, to_mate)

    devices = GROUPS * MEMBERS
    high = lax.broadcasted_iota(jnp.int32, (devices, CS), 0)
    low = lax.broadcasted_iota(jnp.int32, (CS, CS), 0)
    one, zero = jnp.ones((), F32), jnp.zeros((), F32)

    def hot(k, carry):
        at = pl.multiple_of(k * CS, CS)
        for m in range(4):
            q = params[pl.ds(m, 1), pl.ds(at, CS)]
            owner = q // CS
            owner = (owner % MEMBERS) * GROUPS + owner // MEMBERS
            high_hot[k, :, m * CS : m * CS + CS] = jnp.where(high == owner, one, zero).astype(BF16)
            low_hot[k, :, m * CS : m * CS + CS] = jnp.where(low == q % CS, one, zero).astype(BF16)
        return carry

    lax.fori_loop(0, CG // 2, hot, 0)
    got_w(2)
    got_w(1)
    got_x(1)
    got_x(2)
    lax.fori_loop(CG // 2, CG, hot, 0)
    got_w(3)
    got_side(0)
    to_lists.wait()
    keep[0].wait()
    keep[2].wait()
    keep[3].wait()
    for i in range(4):
        garrived(wo.at[:, :, mates[i]], 14 + i)

    xr = xo.reshape(3 * CG, 2, MEMBERS * COLS, CS)
    wr = wo.reshape(CG, 2, MEMBERS * COLS, CS)
    parts = part.reshape(WIDE, 2, MEMBERS * COLS, CS)
    lane = lax.broadcasted_iota(jnp.int32, (1, 256), 1)

    def decode(t):
        b = t % 128
        q = (t // 128) % 128
        r = (t // 16384) % 64
        fresh = (t // (1 << 20)) % 2
        return b, jnp.minimum(q, 3 * CG - 1), jnp.minimum(r, CG - 1), (1 - fresh).astype(F32)

    def far_group(g, run, forward):
        got_t = [decode(lists[1 if forward else 0, 4 * g + i]) for i in range(4)]
        keepers = [((lane // 64 == i) & (lane % RANK < lists[4, got_t[i][0]])).astype(F32) for i in range(4)]
        vm = jnp.concatenate([real_form(v_ref, t[0], -1) for t in got_t], axis=0)
        um = jnp.concatenate([real_form(u_ref, t[0], 1) for t in got_t], axis=0)
        if forward:
            src = jnp.concatenate([rows(xr, t[1], False) for t in got_t], axis=0)
            inner, outer = vm, um
        else:
            src = jnp.concatenate([rows(wr, t[2], True) for t in got_t], axis=0)
            inner, outer = um, vm
        m = mm(src, inner, NT)
        m = jnp.concatenate([(m[32 * i : 32 * i + 32] * keepers[i]).astype(BF16) for i in range(4)], axis=0)
        z = mm(m, outer, NN)
        for i in range(4):
            run = z[32 * i : 32 * i + 32] + got_t[i][3] * run
            prod[4 * g + i] = run
        return run

    def near_block(i, run, forward):
        b, q, r, cont = decode(lists[3 if forward else 2, i])
        b = jnp.minimum(b, NEAR - 1)
        nm = real_form(n_ref, b, -1)
        z = mm(rows(xr, q, False), nm, NT) if forward else mm(rows(wr, r, True), nm, NN)
        run = z + cont * run
        nprod[i] = run
        return run

    blank = jnp.zeros((MEMBERS * COLS, 2 * CS), F32)
    FU, NU = 2, 4

    def far_segment(seg, run, forward):
        n = FAR // 4 // SEGS // FU

        def step(i, run):
            for h in range(FU):
                run = far_group((seg * n + i) * FU + h, run, forward)
            return run

        return lax.fori_loop(0, n, step, run)

    def near_all(forward):
        def step(i, run):
            for h in range(NU):
                run = near_block(i * NU + h, run, forward)
            return run

        lax.fori_loop(0, NEAR // NU, step, blank)

    def collect(lo, hi, shift, far_end, near_end):
        def step(i, carry):
            for h in range(4):
                k = lo + i * 4 + h
                e, n = lists[far_end, k + shift], lists[near_end, k + shift]
                a = prod[jnp.maximum(e - 1, 0)] * jnp.minimum(e, 1).astype(F32)
                a = a + nprod[jnp.clip(n - 1, 0, NEAR - 1)] * jnp.minimum(n, 1).astype(F32)
                parts[k, 0] = a[:, :CS]
                parts[k, 1] = a[:, CS:]
            return carry

        lax.fori_loop(0, (hi - lo) // 4, step, 0)

    run = far_segment(0, blank, False)
    got_x(3)
    run = far_segment(1, run, False)
    got_side(1)
    run = far_segment(2, run, False)
    got_side(2)
    run = far_segment(3, run, False)
    got_side(3)
    keep[4].wait()
    near_all(False)

    def copy(src, dst, k, peer):
        return pltpu.make_async_remote_copy(
            src_ref=src, dst_ref=dst, send_sem=send.at[k], recv_sem=recv.at[k], device_id=peer, device_id_type=MESH
        )

    def go(src, dst, k, peer):
        d = copy(src, dst, k, peer)
        d.start()
        started.append(d)

    def arrived(ref, k):
        copy(ref, ref, k, to_mate).wait_recv()

    tos = [far, up, down, y]
    chunk = 8

    def to_the_mate(ph):
        at = pl.ds(*PHASES[ph])
        for j in range(4):
            go(part.at[at, :, 2 * tos[j] + 1 - p], mate_in.at[j, at], 10 * ph + j, to_mate)

    def pair_sum(j, lo, n, extra=None):
        who = 2 * tos[j] + p

        def step(i, carry):
            at = pl.ds(lo + i * chunk, chunk)
            a = part[at, :, who] + mate_in[j, at]
            if extra is not None:
                a = a + pass_in[extra, at].astype(F32)
            mine[j, at] = a.astype(BF16)
            return carry

        lax.fori_loop(0, n // chunk, step, 0)

    def halves(ph):
        lo, n = PHASES[ph]
        n = n // 2
        return lo, lo + n, n, pl.ds(lo, n), pl.ds(lo + n, n), 10 * ph + 4

    def open_phase(ph):
        a, b, n, at_a, at_b, k = halves(ph)
        everything = pl.ds(*PHASES[ph])
        arrived(mate_in.at[0, everything], 10 * ph)
        pair_sum(0, a, n)
        go(mine.at[0, at_a], pass_in.at[0, at_a], k, to_up)
        pair_sum(0, b, n)
        go(mine.at[0, at_b], pass_in.at[1, at_b], k + 1, to_down)
        arrived(mate_in.at[1, everything], 10 * ph + 1)
        pair_sum(1, b, n)
        go(mine.at[1, at_b], done_in.at[0, at_b], k + 2, to_up)
        arrived(mate_in.at[2, everything], 10 * ph + 2)
        pair_sum(2, a, n)
        go(mine.at[2, at_a], done_in.at[1, at_a], k + 3, to_down)

    def pass_phase(ph):
        a, b, n, at_a, at_b, k = halves(ph)
        arrived(pass_in.at[0, at_a], k)
        pair_sum(1, a, n, 0)
        go(mine.at[1, at_a], done_in.at[0, at_a], k + 4, to_up)
        arrived(pass_in.at[1, at_b], k + 1)
        pair_sum(2, b, n, 1)
        go(mine.at[2, at_b], done_in.at[1, at_b], k + 5, to_down)

    def close_phase(ph):
        a, b, n, at_a, at_b, k = halves(ph)
        arrived(mate_in.at[3, pl.ds(*PHASES[ph])], 10 * ph + 3)
        arrived(done_in.at[0, at_b], k + 2)
        arrived(done_in.at[1, at_a], k + 3)
        arrived(done_in.at[0, at_a], k + 4)
        arrived(done_in.at[1, at_b], k + 5)

    def whole(at):
        a = part[at, :, s] + mate_in[3, at]
        return a + done_in[0, at].astype(F32) + done_in[1, at].astype(F32)

    collect(0, CG, 0, 5, 7)
    collect(CG, 2 * CG, CG, 5, 7)
    to_the_mate(0)
    collect(2 * CG, 3 * CG, -CG, 5, 7)
    to_the_mate(1)
    open_phase(0)
    keep[1].wait()
    for i in range(4):
        garrived(xo.at[own, :, mates[i]], 18 + i)
        garrived(xo.at[left_x, :, mates[i]], 22 + i)
        garrived(xo.at[right_x, :, mates[i]], 26 + i)
    open_phase(1)

    run = far_segment(0, blank, True)
    run = far_segment(1, run, True)
    pass_phase(0)
    run = far_segment(2, run, True)
    pass_phase(1)
    run = far_segment(3, run, True)
    near_all(True)
    collect(3 * CG, 4 * CG, -3 * CG, 6, 8)
    to_the_mate(2)
    close_phase(0)

    def edge(i, carry):
        at = pl.ds(i * chunk, chunk)
        side_out[at] = whole(at)
        return carry

    lax.fori_loop(0, CG // chunk, edge, 0)
    go(side_out.at[pl.ds(0, CG)], side_in.at[0], 30, to_prev)
    lax.fori_loop(CG // chunk, 2 * CG // chunk, edge, 0)
    go(side_out.at[pl.ds(CG, CG)], side_in.at[1], 31, to_next)
    open_phase(2)
    close_phase(1)
    pass_phase(2)
    arrived(side_in.at[0], 30)
    arrived(side_in.at[1], 31)

    def own_adjoint(i, carry):
        at = i * chunk
        here = pl.ds(at, chunk)
        a = whole(pl.ds(2 * CG + at, chunk)) + side_in[0, here] + side_in[1, here]
        adj[here, 0] = a[:, 0]
        adj[here, 1] = -a[:, 1]
        return carry

    lax.fori_loop(0, CG // chunk, own_adjoint, 0)
    close_phase(2)

    def last(i, carry):
        here = pl.ds(i * chunk, chunk)
        f = whole(pl.ds(3 * CG + i * chunk, chunk))
        fwd[here] = f
        prd = f[:, 0] * adj[here, 0] - f[:, 1] * adj[here, 1]
        sens[here] = jnp.sum(prd, axis=1) * (1.0 / (MEMBERS * COLS))
        return carry

    lax.fori_loop(0, CG // chunk, last, 0)

    def cluster(k, carry):
        at = pl.multiple_of(k * CS, CS)
        value = sens[pl.ds(k, 1), :]
        count = counts[pl.ds(k, 1), :]
        tops, rests = [], []
        for m in range(4):
            wt = weights[pl.ds(m, 1), pl.ds(at, CS)]
            val = jnp.where(count > m, wt * value, zero)
            top = val.astype(BF16).astype(F32)
            here = low_hot[k, :, m * CS : m * CS + CS]
            tops.append(here * jnp.broadcast_to(top, (CS, CS)).astype(BF16))
            rests.append(here * jnp.broadcast_to(val - top, (CS, CS)).astype(BF16))
        hits = jnp.concatenate([jnp.concatenate(tops, axis=1), jnp.concatenate(rests, axis=1)], axis=0)
        g = mm(high_hot[k], hits, NT)
        return carry + (g[:, :CS] + g[:, CS:])

    grid[...] = lax.fori_loop(0, CG, cluster, jnp.zeros((devices, CS), F32))

    def part_of(member):
        return grid.at[pl.ds(pl.multiple_of(member * GROUPS, GROUPS), GROUPS)]

    sent = []
    for off in range(1, MEMBERS):
        to = (s + off) % MEMBERS
        d = pltpu.make_async_remote_copy(
            src_ref=part_of(to), dst_ref=got.at[off - 1], send_sem=psend.at[off - 1], recv_sem=precv.at[off - 1],
            device_id={"sub": to}, device_id_type=MESH,
        )
        d.start()
        sent.append(d)
    all_rows = grid[pl.ds(pl.multiple_of(s * GROUPS, GROUPS), GROUPS), :]
    for d in sent:
        d.wait_recv()
    for off in range(MEMBERS - 1):
        all_rows = all_rows + got[off]
    for k in range(GROUPS):
        row[k] = all_rows[k : k + 1]

    def ccopy(off):
        return pltpu.make_async_remote_copy(
            src_ref=row.at[(c + off) % GROUPS], dst_ref=ring.at[off - 1], send_sem=csend.at[off - 1],
            recv_sem=crecv.at[off - 1], device_id={"clus": (c + off) % GROUPS}, device_id_type=MESH,
        )

    def start(off, carry):
        ccopy(off).start()
        return carry

    def wait(off, carry):
        ccopy(off).wait()
        return carry

    lax.fori_loop(1, GROUPS, start, 0)
    for d in sent + started:
        d.wait_send()
    lax.fori_loop(1, GROUPS, wait, 0)
    final = row[c]
    for k in range(GROUPS - 1):
        final = final + ring[k]
    grad[...] = final


ANY = pl.BlockSpec(memory_space=pl.ANY)
VMEM = pl.BlockSpec(memory_space=pltpu.VMEM)


def split_form(x):
    n = x.shape[0]
    return x.reshape(n, COLS, 2, CS).transpose(0, 2, 1, 3)


def joined(x):
    n = x.shape[0]
    return x.transpose(0, 2, 1, 3).reshape(n, COLS, 2 * CS)


def shards(x, w, far_ids, ranks, far_left, far_right, near_ids, near, params, weights, counts):
    def sems(n):
        return pltpu.SemaphoreType.DMA((n,))

    half = (2, COLS, CS)
    fwd, adj, grad = pl.pallas_call(
        kernel,
        out_shape=(
            jax.ShapeDtypeStruct((CG,) + half, F32),
            jax.ShapeDtypeStruct((CG,) + half, F32),
            jax.ShapeDtypeStruct((1, CS), F32),
        ),
        in_specs=[ANY] * 5 + [VMEM] * 6,
        out_specs=(VMEM, VMEM, VMEM),
        scratch_shapes=[
            pltpu.VMEM((3 * CG, 2, MEMBERS, COLS, CS), BF16),
            pltpu.VMEM((CG, 2, MEMBERS, COLS, CS), BF16),
            pltpu.VMEM((FAR, 2, RANK, CS), BF16),
            pltpu.VMEM((FAR, 2, RANK, CS), BF16),
            pltpu.VMEM((NEAR, 2, CS, CS), BF16),
            pltpu.VMEM((8, FAR), jnp.int32),
            pltpu.VMEM((16, FAR), jnp.int32),
            pltpu.SMEM((16, FAR), jnp.int32),
            pltpu.VMEM((FAR, MEMBERS * COLS, 2 * CS), F32),
            pltpu.VMEM((NEAR, MEMBERS * COLS, 2 * CS), F32),
            pltpu.VMEM((WIDE, 2, MEMBERS, COLS, CS), F32),
            pltpu.VMEM((4, WIDE) + half, F32),
            pltpu.VMEM((3, WIDE) + half, BF16),
            pltpu.VMEM((2, WIDE) + half, BF16),
            pltpu.VMEM((2, WIDE) + half, BF16),
            pltpu.VMEM((2 * CG,) + half, F32),
            pltpu.VMEM((2, CG) + half, F32),
            pltpu.VMEM((CG, CS), F32),
            pltpu.VMEM((CG, GROUPS * MEMBERS, 4 * CS), BF16),
            pltpu.VMEM((CG, CS, 4 * CS), BF16),
            pltpu.VMEM((GROUPS * MEMBERS, CS), F32),
            pltpu.VMEM((MEMBERS - 1, GROUPS, CS), F32),
            pltpu.VMEM((GROUPS, 1, CS), F32),
            pltpu.VMEM((GROUPS - 1, 1, CS), F32),
            sems(6),
            sems(30),
            sems(30),
            sems(32),
            sems(32),
            sems(MEMBERS - 1),
            sems(MEMBERS - 1),
            sems(GROUPS - 1),
            sems(GROUPS - 1),
        ],
        compiler_params=pltpu.CompilerParams(collective_id=0, has_side_effects=True, vmem_limit_bytes=60 << 20),
        name="operator",
    )(
        split_form(x), split_form(w), far_left, far_right, near, far_ids, ranks.reshape(1, FAR), near_ids,
        params, weights, counts.reshape(CG, CS),
    )
    return joined(fwd), joined(adj), grad.reshape(CS)


def solution(mesh):
    rhs = P("clus", "sub", None)
    blocks = P(("clus", "sub"), None, None, None)
    both = ("clus", "sub")
    in_specs = (rhs, rhs, P(None, both), P(both), blocks, blocks, P(None, both), blocks)
    in_specs += (P(None, "clus"), P(None, "clus"), P("clus"))
    out_specs = (rhs, rhs, P(both))
    return jax.shard_map(shards, mesh=mesh, in_specs=in_specs, out_specs=out_specs, check_vma=False)
```

time: 564 us -> 78.7 us (0.14)
  waiting for transfers between devices: 297 us -> 0 us
  other arithmetic: 149 us -> 0 us
  Pallas kernels: 0 us -> 73.6 us
  local copies, waits for them, and re-layouts: 33.8 us -> 4.26 us
  blocking collectives: 29.5 us -> 0 us
  matrix products: 29.3 us -> 0 us
  between operations: 14.2 us -> 0.64 us
  starting transfers between devices: 8.78 us -> 0 us
    unnamed x4 -> x0, waiting for transfers between devices: 243 us -> none
    scatter-add x5 -> x0, other arithmetic: 130 us -> none  [the longest x1 93.3 us: shards(): jax.ops.segment_sum(weighted.reshape(-1), panel_params.reshape(-1), num_s...]
    pallas_call x0 -> x1, Pallas kernels: none -> 73.6 us  [shards(): pl.pallas_call(kernel, out_shape=(jax.ShapeDtypeStruct((CG,) + half, F32)...]
    all_gather x2 -> x0, blocking collectives: 29.5 us -> none  [the longest x1 16.1 us: shards(): lax.all_gather(forward_rhs, 'sub', axis=1, tiled=True)]
    dot_general x24 -> x0, matrix products: 29.3 us -> none  [the longest x6 8.23 us: complex_mix(): jnp.einsum(einsum_form, imag_lhs, imag_rhs, preferred_element_type=jnp.fl...]
    ppermute x4 -> x0, waiting for transfers between devices: 27.6 us -> none  [the longest x2 27.6 us: shifted(): lax.ppermute(x, axis, [(i, (i + by) % devices) for i in range(devices)])]
    reduce_scatter x2 -> x0, waiting for transfers between devices: 26.8 us -> none  [the longest x1 26.8 us: shards(): lax.psum_scatter(own_terms, 'sub', scatter_dimension=1, tiled=True)]
    unnamed x59 -> x3, local copies, waits for them, and re-layouts: 16.3 us -> 4.26 us
  transfers between devices with their start and end apart: 7 -> 0, of which waited for: 4 -> 0; matrix products, arithmetic and copies ran while one was open for 10% -> 0% of each run, Pallas kernels for 0% -> 0%
where the time goes in v2:
time: 78.7 us; the launch traced here: 78.5 us
  Pallas kernels  73.6 us (94%)
  local copies, waits for them, and re-layouts  4.26 us (5%)
    pallas_call x1, Pallas kernels, shards(): pl.pallas_call(kernel, out_shape=(jax.ShapeDtypeStruct((CG,) + half, F32)...  73.6 us
    unnamed x3, local copies, waits for them, and re-layouts  4.26 us

profile of v2, /device:TPU:1, one launch (start us, length us, event | category | flops | bytes accessed | tf_op | source)
XLA Modules:
  0.0 78.5 jit_solution(6785494188598845772)
XLA Ops:
  0.6 73.6 %operator.1 = (f32[32,2,4,128]{3,2,1,0:T(4,128)}, f32[32,2,4,128]{3,2,1,0:T(4,128)}, f32[1,128]{1,0:T(1,128)}) custom-call(bf16[32,2,4,128]{3,2,1,0:T(4,128)(2,1)} %bitcast.17, bf16[32,2,4,128]{3,2,1,0:T(4,128)(2,1)} %bitcast.18, bf16[128,2,32,128]{3,2,1,0:T(8,128)(2,1)} %u_hbm.1, bf16[128,2,32,128]{3,2,1,0:T(8,128)(2,1)} %v_hbm.1, ...), custom_call_target="tpu_custom_call" | custom-call | tf_op jit(solution)/shard_map/operator/pallas_call | solution.py:514
  74.3 1.6 %copy.17 = f32[32,4,256]{2,1,0:T(4,128)} copy(f32[32,4,256]{2,1,0:T(4,128)} %bitcast.16) | data formatting | bytes 262144
  75.8 1.6 %copy.18 = f32[32,4,256]{2,1,0:T(4,128)} copy(f32[32,4,256]{2,1,0:T(4,128)} %bitcast.15) | data formatting | bytes 262144
  77.4 1.1 %copy.19 = f32[128]{0:T(128)} copy(f32[128]{0:T(128)} %bitcast.21) | data formatting | bytes 1024

commit v3 on v2

--- a/solution.py
+++ b/solution.py
@@ -18,7 +18,7 @@
 RANK = 32
 FAR = 128
 NEAR = 32
-SEGS = 4
+SEGS = 2
 WIDE = 4 * CG
 
 
@@ -53,6 +53,10 @@
     return jnp.concatenate([re, -im if conj else im], axis=1)
 
 
+def cols(member):
+    return pl.ds(pl.multiple_of(COLS * member, COLS), COLS)
+
+
 PHASES = ((0, 2 * CG), (2 * CG, CG), (3 * CG, CG))
 
 
@@ -60,8 +64,8 @@
     x_ref, w_ref, u_hbm, v_hbm, n_hbm, far_ids, ranks, near_ids, params, weights, counts,
     fwd, adj, grad,
     xo, wo, u_ref, v_ref, n_ref, ids, table, lists, prod, nprod, part, mate_in, mine, pass_in, done_in,
-    side_out, side_in, sens, high_hot, low_hot, grid, got, row, ring,
-    local, gsend, grecv, send, recv, psend, precv, csend, crecv,
+    side_out, side_in, sens, sgot, high_hot, low_hot, grid, got, row, ring,
+    local, gsend, grecv, send, recv, ssend, srecv, psend, precv, csend, crecv,
 ):
     c, s, y, p, up, down, far = place()
     to_up, to_down = {"sub": 2 * up + p}, {"sub": 2 * down + p}
@@ -82,8 +86,8 @@
 
     own = pl.ds(CG, CG)
     keep = [
-        pltpu.make_async_copy(w_ref, wo.at[:, :, s], local.at[0]),
-        pltpu.make_async_copy(x_ref, xo.at[own, :, s], local.at[1]),
+        pltpu.make_async_copy(w_ref, wo.at[:, :, cols(s)], local.at[0]),
+        pltpu.make_async_copy(x_ref, xo.at[own, :, cols(s)], local.at[1]),
         pltpu.make_async_copy(u_hbm, u_ref, local.at[2]),
         pltpu.make_async_copy(v_hbm, v_ref, local.at[3]),
         pltpu.make_async_copy(n_hbm, n_ref, local.at[4]),
@@ -102,7 +106,7 @@
     slot_row = lax.broadcasted_iota(jnp.int32, (1, FAR), 1)
     table[...] = jnp.zeros_like(table)
 
-    def order(key, payload, at, end_at):
+    def order(key, payload, at, end_at, none):
         k = jnp.broadcast_to(key, (FAR, FAR))
         kt = k.T
         tie = (k == kt) & (lane_i < sub_i)
@@ -114,18 +118,41 @@
         table[pl.ds(at, 1), :] = jnp.sum(jnp.where(rank == lane_i, pay, zeros), axis=0, keepdims=True)
         upto = jnp.sum(jnp.where(kt <= lane_i, ones, zeros), axis=0, keepdims=True)
         below = jnp.sum(jnp.where(kt < lane_i, ones, zeros), axis=0, keepdims=True)
-        table[pl.ds(end_at, 1), :] = jnp.where(upto > below, upto, 0)
+        table[pl.ds(end_at, 1), :] = jnp.where(upto > below, upto - 1, none)
 
     for i, count in ((0, FAR), (1, NEAR)):
         live = slot_row < count
         r = jnp.clip(ids[2 * i : 2 * i + 1, :] - first, 0, CG - 1)
         q = jnp.clip((ids[2 * i + 1 : 2 * i + 2, :] - first + CG + total) % total, 0, 3 * CG - 1)
         payload = slot_row + q * 128 + r * 16384
-        order(jnp.where(live, q, big), payload, 2 * i, 5 + 2 * i)
-        order(jnp.where(live, r, big), payload, 2 * i + 1, 6 + 2 * i)
-    table[4:5, :] = ranks[...]
+        if i == 0:
+            payload = payload + (ranks[...] << 21)
+        order(jnp.where(live, q, big), payload, 2 * i, 5 + 2 * i, count)
+        order(jnp.where(live, r, big), payload, 2 * i + 1, 6 + 2 * i, count)
     to_lists = pltpu.make_async_copy(table, lists, local.at[5])
     to_lists.start()
+
+
+    devices = GROUPS * MEMBERS
+    high = lax.broadcasted_iota(jnp.int32, (devices, CS), 0).astype(F32).astype(BF16)
+    low = lax.broadcasted_iota(jnp.int32, (CS, CS), 0).astype(F32).astype(BF16)
+    one, zero = jnp.ones((), BF16), jnp.zeros((), BF16)
+
+    def hot(j, carry):
+        at = pl.multiple_of((4 * s + j) * CS, CS)
+        for m in range(4):
+            q = params[pl.ds(m, 1), pl.ds(at, CS)]
+            owner = q // CS
+            owner = ((owner % MEMBERS) * GROUPS + owner // MEMBERS).astype(F32)
+            below = (q % CS).astype(F32)
+            here = pl.ds(pl.multiple_of((j % 2) * 4 * CS + m * CS, CS), CS)
+            wide = jnp.broadcast_to(owner, (devices, CS)).astype(BF16)
+            high_hot[j // 2, :, here] = jnp.where(high == wide, one, zero)
+            low_hot[j // 2, :, here] = jnp.where(low == wide_of(below), one, zero)
+        return carry
+
+    def wide_of(v):
+        return jnp.broadcast_to(v, (CS, CS)).astype(BF16)
 
     pl.semaphore_wait(barrier, MEMBERS - 1 + GROUPS - 1)
 
@@ -147,94 +174,78 @@
         gcopy(ref, ref, k, to_mate).wait_recv()
 
     left_x, right_x = pl.ds(0, CG), pl.ds(2 * CG, CG)
-    ggo(w_ref, wo.at[:, :, s], 0, to_up)
-    ggo(w_ref, wo.at[:, :, s], 1, to_down)
-    ggo(w_ref, wo.at[:, :, s], 14, to_mate)
-    ggo(x_ref, xo.at[left_x, :, s], 6, to_next)
-    ggo(x_ref, xo.at[right_x, :, s], 10, to_prev)
-    ggo(x_ref, xo.at[own, :, s], 3, to_up)
-    ggo(x_ref, xo.at[own, :, s], 4, to_down)
-    ggo(x_ref, xo.at[own, :, s], 18, to_mate)
+    ggo(w_ref, wo.at[:, :, cols(s)], 0, to_up)
+    ggo(w_ref, wo.at[:, :, cols(s)], 1, to_down)
+    ggo(w_ref, wo.at[:, :, cols(s)], 14, to_mate)
+    ggo(x_ref, xo.at[left_x, :, cols(s)], 6, to_next)
+    ggo(x_ref, xo.at[right_x, :, cols(s)], 10, to_prev)
+    ggo(x_ref, xo.at[own, :, cols(s)], 3, to_up)
+    ggo(x_ref, xo.at[own, :, cols(s)], 4, to_down)
+    ggo(x_ref, xo.at[own, :, cols(s)], 18, to_mate)
 
     def got_w(i):
-        ref = wo.at[:, :, subs[i]]
+        ref = wo.at[:, :, cols(subs[i])]
         garrived(ref, i - 1)
         if i == 2:
             ggo(ref, ref, 2, to_down)
         ggo(ref, ref, 14 + i, to_mate)
 
     def got_x(i):
-        ref = xo.at[own, :, subs[i]]
+        ref = xo.at[own, :, cols(subs[i])]
         garrived(ref, 2 + i)
         if i == 1:
             ggo(ref, ref, 5, to_up)
-        ggo(ref, xo.at[left_x, :, subs[i]], 6 + i, to_next)
-        ggo(ref, xo.at[right_x, :, subs[i]], 10 + i, to_prev)
+        ggo(ref, xo.at[left_x, :, cols(subs[i])], 6 + i, to_next)
+        ggo(ref, xo.at[right_x, :, cols(subs[i])], 10 + i, to_prev)
         ggo(ref, ref, 18 + i, to_mate)
 
     def got_side(i):
-        left = xo.at[left_x, :, subs[i]]
+        left = xo.at[left_x, :, cols(subs[i])]
         garrived(left, 6 + i)
         ggo(left, left, 22 + i, to_mate)
-        right = xo.at[right_x, :, subs[i]]
+        right = xo.at[right_x, :, cols(subs[i])]
         garrived(right, 10 + i)
         ggo(right, right, 26 + i, to_mate)
 
-    devices = GROUPS * MEMBERS
-    high = lax.broadcasted_iota(jnp.int32, (devices, CS), 0)
-    low = lax.broadcasted_iota(jnp.int32, (CS, CS), 0)
-    one, zero = jnp.ones((), F32), jnp.zeros((), F32)
-
-    def hot(k, carry):
-        at = pl.multiple_of(k * CS, CS)
-        for m in range(4):
-            q = params[pl.ds(m, 1), pl.ds(at, CS)]
-            owner = q // CS
-            owner = (owner % MEMBERS) * GROUPS + owner // MEMBERS
-            high_hot[k, :, m * CS : m * CS + CS] = jnp.where(high == owner, one, zero).astype(BF16)
-            low_hot[k, :, m * CS : m * CS + CS] = jnp.where(low == q % CS, one, zero).astype(BF16)
-        return carry
-
-    lax.fori_loop(0, CG // 2, hot, 0)
+    lax.fori_loop(0, 4, hot, 0)
     got_w(2)
     got_w(1)
     got_x(1)
     got_x(2)
-    lax.fori_loop(CG // 2, CG, hot, 0)
+    got_side(0)
     got_w(3)
-    got_side(0)
     to_lists.wait()
     keep[0].wait()
     keep[2].wait()
     keep[3].wait()
     for i in range(4):
-        garrived(wo.at[:, :, mates[i]], 14 + i)
-
-    xr = xo.reshape(3 * CG, 2, MEMBERS * COLS, CS)
-    wr = wo.reshape(CG, 2, MEMBERS * COLS, CS)
+        garrived(wo.at[:, :, cols(mates[i])], 14 + i)
+
+    xr, wr = xo, wo
     parts = part.reshape(WIDE, 2, MEMBERS * COLS, CS)
     lane = lax.broadcasted_iota(jnp.int32, (1, 256), 1)
 
     def decode(t):
-        b = t % 128
-        q = (t // 128) % 128
-        r = (t // 16384) % 64
-        fresh = (t // (1 << 20)) % 2
-        return b, jnp.minimum(q, 3 * CG - 1), jnp.minimum(r, CG - 1), (1 - fresh).astype(F32)
-
-    def far_group(g, run, forward):
+        return t & 127, (t >> 7) & 127, (t >> 14) & 63, (1 - ((t >> 20) & 1)).astype(F32), t >> 21
+
+    def far_inner(g, forward):
         got_t = [decode(lists[1 if forward else 0, 4 * g + i]) for i in range(4)]
-        keepers = [((lane // 64 == i) & (lane % RANK < lists[4, got_t[i][0]])).astype(F32) for i in range(4)]
-        vm = jnp.concatenate([real_form(v_ref, t[0], -1) for t in got_t], axis=0)
-        um = jnp.concatenate([real_form(u_ref, t[0], 1) for t in got_t], axis=0)
+        keepers = [((lane // 64 == i) & (lane % RANK < got_t[i][4])).astype(F32) for i in range(4)]
         if forward:
             src = jnp.concatenate([rows(xr, t[1], False) for t in got_t], axis=0)
-            inner, outer = vm, um
+            inner = jnp.concatenate([real_form(v_ref, t[0], -1) for t in got_t], axis=0)
         else:
             src = jnp.concatenate([rows(wr, t[2], True) for t in got_t], axis=0)
-            inner, outer = um, vm
+            inner = jnp.concatenate([real_form(u_ref, t[0], 1) for t in got_t], axis=0)
         m = mm(src, inner, NT)
         m = jnp.concatenate([(m[32 * i : 32 * i + 32] * keepers[i]).astype(BF16) for i in range(4)], axis=0)
+        return m, got_t
+
+    def far_outer(g, run, m, got_t, forward):
+        if forward:
+            outer = jnp.concatenate([real_form(u_ref, t[0], 1) for t in got_t], axis=0)
+        else:
+            outer = jnp.concatenate([real_form(v_ref, t[0], -1) for t in got_t], axis=0)
         z = mm(m, outer, NN)
         for i in range(4):
             run = z[32 * i : 32 * i + 32] + got_t[i][3] * run
@@ -242,8 +253,7 @@
         return run
 
     def near_block(i, run, forward):
-        b, q, r, cont = decode(lists[3 if forward else 2, i])
-        b = jnp.minimum(b, NEAR - 1)
+        b, q, r, cont, _ = decode(lists[3 if forward else 2, i])
         nm = real_form(n_ref, b, -1)
         z = mm(rows(xr, q, False), nm, NT) if forward else mm(rows(wr, r, True), nm, NN)
         run = z + cont * run
@@ -251,14 +261,18 @@
         return run
 
     blank = jnp.zeros((MEMBERS * COLS, 2 * CS), F32)
-    FU, NU = 2, 4
+    prod[FAR] = blank
+    nprod[NEAR] = blank
+    FU, NU = 8, 8
 
     def far_segment(seg, run, forward):
         n = FAR // 4 // SEGS // FU
 
         def step(i, run):
-            for h in range(FU):
-                run = far_group((seg * n + i) * FU + h, run, forward)
+            at = [(seg * n + i) * FU + h for h in range(FU)]
+            inner = [far_inner(g, forward) for g in at]
+            for g, (m, got_t) in zip(at, inner):
+                run = far_outer(g, run, m, got_t, forward)
             return run
 
         return lax.fori_loop(0, n, step, run)
@@ -275,9 +289,7 @@
         def step(i, carry):
             for h in range(4):
                 k = lo + i * 4 + h
-                e, n = lists[far_end, k + shift], lists[near_end, k + shift]
-                a = prod[jnp.maximum(e - 1, 0)] * jnp.minimum(e, 1).astype(F32)
-                a = a + nprod[jnp.clip(n - 1, 0, NEAR - 1)] * jnp.minimum(n, 1).astype(F32)
+                a = prod[lists[far_end, k + shift]] + nprod[lists[near_end, k + shift]]
                 parts[k, 0] = a[:, :CS]
                 parts[k, 1] = a[:, CS:]
             return carry
@@ -286,12 +298,8 @@
 
     run = far_segment(0, blank, False)
     got_x(3)
-    run = far_segment(1, run, False)
+    far_segment(1, run, False)
     got_side(1)
-    run = far_segment(2, run, False)
-    got_side(2)
-    run = far_segment(3, run, False)
-    got_side(3)
     keep[4].wait()
     near_all(False)
 
@@ -373,22 +381,22 @@
     collect(0, CG, 0, 5, 7)
     collect(CG, 2 * CG, CG, 5, 7)
     to_the_mate(0)
+    got_side(2)
     collect(2 * CG, 3 * CG, -CG, 5, 7)
     to_the_mate(1)
     open_phase(0)
+    got_side(3)
+    open_phase(1)
     keep[1].wait()
     for i in range(4):
-        garrived(xo.at[own, :, mates[i]], 18 + i)
-        garrived(xo.at[left_x, :, mates[i]], 22 + i)
-        garrived(xo.at[right_x, :, mates[i]], 26 + i)
-    open_phase(1)
+        garrived(xo.at[own, :, cols(mates[i])], 18 + i)
+        garrived(xo.at[left_x, :, cols(mates[i])], 22 + i)
+        garrived(xo.at[right_x, :, cols(mates[i])], 26 + i)
 
     run = far_segment(0, blank, True)
-    run = far_segment(1, run, True)
     pass_phase(0)
-    run = far_segment(2, run, True)
+    far_segment(1, run, True)
     pass_phase(1)
-    run = far_segment(3, run, True)
     near_all(True)
     collect(3 * CG, 4 * CG, -3 * CG, 6, 8)
     to_the_mate(2)
@@ -425,43 +433,61 @@
         f = whole(pl.ds(3 * CG + i * chunk, chunk))
         fwd[here] = f
         prd = f[:, 0] * adj[here, 0] - f[:, 1] * adj[here, 1]
-        sens[here] = jnp.sum(prd, axis=1) * (1.0 / (MEMBERS * COLS))
+        both = jnp.sum(prd, axis=1) * (1.0 / (MEMBERS * COLS))
+        sens[2 * i] = both[:COLS]
+        sens[2 * i + 1] = both[COLS:]
         return carry
 
     lax.fori_loop(0, CG // chunk, last, 0)
 
-    def cluster(k, carry):
-        at = pl.multiple_of(k * CS, CS)
-        value = sens[pl.ds(k, 1), :]
-        count = counts[pl.ds(k, 1), :]
+    sent = []
+
+    def spread(src_of, dst, sems_out, sems_in):
+        out = []
+        for off in range(1, MEMBERS):
+            to = (s + off) % MEMBERS
+            d = pltpu.make_async_remote_copy(
+                src_ref=src_of(to), dst_ref=dst.at[off - 1], send_sem=sems_out.at[off - 1],
+                recv_sem=sems_in.at[off - 1], device_id={"sub": to}, device_id_type=MESH,
+            )
+            d.start()
+            out.append(d)
+        sent.extend(out)
+        return out
+
+    for d in spread(lambda to: sens.at[to], sgot, ssend, srecv):
+        d.wait_recv()
+    value = sens[s]
+    for off in range(MEMBERS - 1):
+        value = value + sgot[off]
+    counted = counts[pl.ds(pl.multiple_of(4 * s, 4), 4), :]
+    total_grid = None
+    for k in range(2):
         tops, rests = [], []
-        for m in range(4):
-            wt = weights[pl.ds(m, 1), pl.ds(at, CS)]
-            val = jnp.where(count > m, wt * value, zero)
-            top = val.astype(BF16).astype(F32)
-            here = low_hot[k, :, m * CS : m * CS + CS]
-            tops.append(here * jnp.broadcast_to(top, (CS, CS)).astype(BF16))
-            rests.append(here * jnp.broadcast_to(val - top, (CS, CS)).astype(BF16))
+        for h in range(2):
+            j = 2 * k + h
+            at = pl.multiple_of((4 * s + j) * CS, CS)
+            for m in range(4):
+                wt = weights[pl.ds(m, 1), pl.ds(at, CS)]
+                val = wt * value[j : j + 1]
+                val = jnp.where(counted[j : j + 1] > m, val, jnp.zeros_like(val))
+                top = val.astype(BF16).astype(F32)
+                lo = (4 * h + m) * CS
+                here = low_hot[k, :, lo : lo + CS]
+                tops.append(here * wide_of(top))
+                rests.append(here * wide_of(val - top))
         hits = jnp.concatenate([jnp.concatenate(tops, axis=1), jnp.concatenate(rests, axis=1)], axis=0)
         g = mm(high_hot[k], hits, NT)
-        return carry + (g[:, :CS] + g[:, CS:])
-
-    grid[...] = lax.fori_loop(0, CG, cluster, jnp.zeros((devices, CS), F32))
+        g = g[:, :CS] + g[:, CS:]
+        total_grid = g if k == 0 else total_grid + g
+    grid[...] = total_grid
 
     def part_of(member):
         return grid.at[pl.ds(pl.multiple_of(member * GROUPS, GROUPS), GROUPS)]
 
-    sent = []
-    for off in range(1, MEMBERS):
-        to = (s + off) % MEMBERS
-        d = pltpu.make_async_remote_copy(
-            src_ref=part_of(to), dst_ref=got.at[off - 1], send_sem=psend.at[off - 1], recv_sem=precv.at[off - 1],
-            device_id={"sub": to}, device_id_type=MESH,
-        )
-        d.start()
-        sent.append(d)
+    arrivals = spread(part_of, got, psend, precv)
     all_rows = grid[pl.ds(pl.multiple_of(s * GROUPS, GROUPS), GROUPS), :]
-    for d in sent:
+    for d in arrivals:
         d.wait_recv()
     for off in range(MEMBERS - 1):
         all_rows = all_rows + got[off]
@@ -490,6 +516,12 @@
     for k in range(GROUPS - 1):
         final = final + ring[k]
     grad[...] = final
+
+
+def hand_out(a, b, c, x, y, z):
+    x[...] = a[...]
+    y[...] = b[...]
+    z[...] = c[...]
 
 
 ANY = pl.BlockSpec(memory_space=pl.ANY)
@@ -521,16 +553,16 @@
         in_specs=[ANY] * 5 + [VMEM] * 6,
         out_specs=(VMEM, VMEM, VMEM),
         scratch_shapes=[
-            pltpu.VMEM((3 * CG, 2, MEMBERS, COLS, CS), BF16),
-            pltpu.VMEM((CG, 2, MEMBERS, COLS, CS), BF16),
+            pltpu.VMEM((3 * CG, 2, MEMBERS * COLS, CS), BF16),
+            pltpu.VMEM((CG, 2, MEMBERS * COLS, CS), BF16),
             pltpu.VMEM((FAR, 2, RANK, CS), BF16),
             pltpu.VMEM((FAR, 2, RANK, CS), BF16),
             pltpu.VMEM((NEAR, 2, CS, CS), BF16),
             pltpu.VMEM((8, FAR), jnp.int32),
             pltpu.VMEM((16, FAR), jnp.int32),
             pltpu.SMEM((16, FAR), jnp.int32),
-            pltpu.VMEM((FAR, MEMBERS * COLS, 2 * CS), F32),
-            pltpu.VMEM((NEAR, MEMBERS * COLS, 2 * CS), F32),
+            pltpu.VMEM((FAR + 1, MEMBERS * COLS, 2 * CS), F32),
+            pltpu.VMEM((NEAR + 1, MEMBERS * COLS, 2 * CS), F32),
             pltpu.VMEM((WIDE, 2, MEMBERS, COLS, CS), F32),
             pltpu.VMEM((4, WIDE) + half, F32),
             pltpu.VMEM((3, WIDE) + half, BF16),
@@ -538,9 +570,10 @@
             pltpu.VMEM((2, WIDE) + half, BF16),
             pltpu.VMEM((2 * CG,) + half, F32),
             pltpu.VMEM((2, CG) + half, F32),
-            pltpu.VMEM((CG, CS), F32),
-            pltpu.VMEM((CG, GROUPS * MEMBERS, 4 * CS), BF16),
-            pltpu.VMEM((CG, CS, 4 * CS), BF16),
+            pltpu.VMEM((MEMBERS, COLS, CS), F32),
+            pltpu.VMEM((MEMBERS - 1, COLS, CS), F32),
+            pltpu.VMEM((2, GROUPS * MEMBERS, 8 * CS), BF16),
+            pltpu.VMEM((2, CS, 8 * CS), BF16),
             pltpu.VMEM((GROUPS * MEMBERS, CS), F32),
             pltpu.VMEM((MEMBERS - 1, GROUPS, CS), F32),
             pltpu.VMEM((GROUPS, 1, CS), F32),
@@ -552,6 +585,8 @@
             sems(32),
             sems(MEMBERS - 1),
             sems(MEMBERS - 1),
+            sems(MEMBERS - 1),
+            sems(MEMBERS - 1),
             sems(GROUPS - 1),
             sems(GROUPS - 1),
         ],
@@ -561,6 +596,13 @@
         split_form(x), split_form(w), far_left, far_right, near, far_ids, ranks.reshape(1, FAR), near_ids,
         params, weights, counts.reshape(CG, CS),
     )
+    fwd, adj, grad = pl.pallas_call(
+        hand_out,
+        out_shape=tuple(jax.ShapeDtypeStruct(a.shape, a.dtype) for a in (fwd, adj, grad)),
+        in_specs=[VMEM] * 3,
+        out_specs=(VMEM,) * 3,
+        name="hand_out",
+    )(fwd, adj, grad)
     return joined(fwd), joined(adj), grad.reshape(CS)
 
 

time: 78.7 us -> 59.2 us (0.75)
  Pallas kernels: 73.6 us -> 58.4 us
  local copies, waits for them, and re-layouts: 4.26 us -> 0 us
    pallas_call x1, Pallas kernels: 73.6 us -> 56.7 us  [shards(): pl.pallas_call(kernel, out_shape=(jax.ShapeDtypeStruct((CG,) + half, F32)...]
    unnamed x3 -> x0, local copies, waits for them, and re-layouts: 4.26 us -> none
    pallas_call x0 -> x1, Pallas kernels: none -> 1.68 us  [shards(): pl.pallas_call(hand_out, out_shape=tuple((jax.ShapeDtypeStruct(a.shape, a...]
where the time goes in v3:
time: 59.2 us; the launch traced here: 59 us
  Pallas kernels  58.4 us (99%)
  between operations  0.64 us (1%)
    pallas_call x1, Pallas kernels, shards(): pl.pallas_call(kernel, out_shape=(jax.ShapeDtypeStruct((CG,) + half, F32)...  56.7 us
    pallas_call x1, Pallas kernels, shards(): pl.pallas_call(hand_out, out_shape=tuple((jax.ShapeDtypeStruct(a.shape, a...  1.68 us

profile of v3, /device:TPU:1, one launch (start us, length us, event | category | flops | bytes accessed | tf_op | source)
XLA Modules:
  0.0 59.0 jit_solution(1422826172772964362)
XLA Ops:
  0.6 56.7 %operator.1 = (f32[32,2,4,128]{3,2,1,0:T(4,128)}, f32[32,2,4,128]{3,2,1,0:T(4,128)}, f32[1,128]{1,0:T(1,128)}) custom-call(bf16[32,2,4,128]{3,2,1,0:T(4,128)(2,1)} %bitcast.15, bf16[32,2,4,128]{3,2,1,0:T(4,128)(2,1)} %bitcast.16, bf16[128,2,32,128]{3,2,1,0:T(8,128)(2,1)} %u_hbm.1, bf16[128,2,32,128]{3,2,1,0:T(8,128)(2,1)} %v_hbm.1, ...), custom_call_target="tpu_custom_call" | custom-call | tf_op jit(solution)/shard_map/operator/pallas_call | solution.py:546
  57.4 1.7 %hand_out.1 = (f32[32,2,4,128]{3,2,1,0:T(4,128)}, f32[32,2,4,128]{3,2,1,0:T(4,128)}, f32[1,128]{1,0:T(1,128)}) custom-call(f32[32,2,4,128]{3,2,1,0:T(4,128)} %get-tuple-element.9.a, f32[32,2,4,128]{3,2,1,0:T(4,128)} %get-tuple-element.10.b, f32[1,128]{1,0:T(1,128)} %get-tuple-element.11.c), custom_call_target="tpu_custom_call" | custom-call | tf_op jit(solution)/shard_map/hand_out/pallas_call | solution.py:599

commit v4 on v3

--- a/solution.py
+++ b/solution.py
@@ -64,12 +64,12 @@
     x_ref, w_ref, u_hbm, v_hbm, n_hbm, far_ids, ranks, near_ids, params, weights, counts,
     fwd, adj, grad,
     xo, wo, u_ref, v_ref, n_ref, ids, table, lists, prod, nprod, part, mate_in, mine, pass_in, done_in,
-    side_out, side_in, sens, sgot, high_hot, low_hot, grid, got, row, ring,
-    local, gsend, grecv, send, recv, ssend, srecv, psend, precv, csend, crecv,
+    side_out, side_in, sens, sgot, summed, high_hot, low_hot, row, ring,
+    local, gsend, grecv, send, recv, ssend, srecv, csend, crecv,
 ):
     c, s, y, p, up, down, far = place()
     to_up, to_down = {"sub": 2 * up + p}, {"sub": 2 * down + p}
-    to_mate = {"sub": 2 * y + 1 - p}
+    to_mate, to_far = {"sub": 2 * y + 1 - p}, {"sub": 2 * far + p}
     to_next, to_prev = {"clus": (c + 1) % GROUPS}, {"clus": (c + GROUPS - 1) % GROUPS}
     barrier = pltpu.get_barrier_semaphore()
 
@@ -133,26 +133,22 @@
     to_lists.start()
 
 
-    devices = GROUPS * MEMBERS
-    high = lax.broadcasted_iota(jnp.int32, (devices, CS), 0).astype(F32).astype(BF16)
+    high = (lax.broadcasted_iota(jnp.int32, (GROUPS, CS), 0) * MEMBERS + s).astype(F32).astype(BF16)
     low = lax.broadcasted_iota(jnp.int32, (CS, CS), 0).astype(F32).astype(BF16)
     one, zero = jnp.ones((), BF16), jnp.zeros((), BF16)
 
-    def hot(j, carry):
-        at = pl.multiple_of((4 * s + j) * CS, CS)
+    def hot(k, carry):
+        at = pl.multiple_of(k * CS, CS)
         for m in range(4):
             q = params[pl.ds(m, 1), pl.ds(at, CS)]
-            owner = q // CS
-            owner = ((owner % MEMBERS) * GROUPS + owner // MEMBERS).astype(F32)
-            below = (q % CS).astype(F32)
-            here = pl.ds(pl.multiple_of((j % 2) * 4 * CS + m * CS, CS), CS)
-            wide = jnp.broadcast_to(owner, (devices, CS)).astype(BF16)
-            high_hot[j // 2, :, here] = jnp.where(high == wide, one, zero)
-            low_hot[j // 2, :, here] = jnp.where(low == wide_of(below), one, zero)
-        return carry
-
-    def wide_of(v):
-        return jnp.broadcast_to(v, (CS, CS)).astype(BF16)
+            here = slice(m * CS, m * CS + CS)
+            owner = (q // CS).astype(F32)
+            high_hot[k, :, here] = jnp.where(high == wide_of(owner, GROUPS), one, zero)
+            low_hot[k, :, here] = jnp.where(low == wide_of((q % CS).astype(F32), CS), one, zero)
+        return carry
+
+    def wide_of(v, n):
+        return jnp.broadcast_to(v, (n, CS)).astype(BF16)
 
     pl.semaphore_wait(barrier, MEMBERS - 1 + GROUPS - 1)
 
@@ -174,20 +170,19 @@
         gcopy(ref, ref, k, to_mate).wait_recv()
 
     left_x, right_x = pl.ds(0, CG), pl.ds(2 * CG, CG)
-    ggo(w_ref, wo.at[:, :, cols(s)], 0, to_up)
-    ggo(w_ref, wo.at[:, :, cols(s)], 1, to_down)
-    ggo(w_ref, wo.at[:, :, cols(s)], 14, to_mate)
+    ggo(w_ref, wo.at[:, :, cols(s)], 2, to_far)
     ggo(x_ref, xo.at[left_x, :, cols(s)], 6, to_next)
     ggo(x_ref, xo.at[right_x, :, cols(s)], 10, to_prev)
     ggo(x_ref, xo.at[own, :, cols(s)], 3, to_up)
+    ggo(w_ref, wo.at[:, :, cols(s)], 1, to_down)
+    ggo(w_ref, wo.at[:, :, cols(s)], 0, to_up)
     ggo(x_ref, xo.at[own, :, cols(s)], 4, to_down)
+    ggo(w_ref, wo.at[:, :, cols(s)], 14, to_mate)
     ggo(x_ref, xo.at[own, :, cols(s)], 18, to_mate)
 
     def got_w(i):
         ref = wo.at[:, :, cols(subs[i])]
         garrived(ref, i - 1)
-        if i == 2:
-            ggo(ref, ref, 2, to_down)
         ggo(ref, ref, 14 + i, to_mate)
 
     def got_x(i):
@@ -207,13 +202,14 @@
         garrived(right, 10 + i)
         ggo(right, right, 26 + i, to_mate)
 
-    lax.fori_loop(0, 4, hot, 0)
+    lax.fori_loop(0, 3 * CG // 4, hot, 0)
+    got_side(0)
+    lax.fori_loop(3 * CG // 4, CG, hot, 0)
+    got_x(1)
     got_w(2)
+    got_w(3)
+    got_x(2)
     got_w(1)
-    got_x(1)
-    got_x(2)
-    got_side(0)
-    got_w(3)
     to_lists.wait()
     keep[0].wait()
     keep[2].wait()
@@ -252,13 +248,10 @@
             prod[4 * g + i] = run
         return run
 
-    def near_block(i, run, forward):
+    def near_product(i, forward):
         b, q, r, cont, _ = decode(lists[3 if forward else 2, i])
         nm = real_form(n_ref, b, -1)
-        z = mm(rows(xr, q, False), nm, NT) if forward else mm(rows(wr, r, True), nm, NN)
-        run = z + cont * run
-        nprod[i] = run
-        return run
+        return (mm(rows(xr, q, False), nm, NT) if forward else mm(rows(wr, r, True), nm, NN)), cont
 
     blank = jnp.zeros((MEMBERS * COLS, 2 * CS), F32)
     prod[FAR] = blank
@@ -279,8 +272,10 @@
 
     def near_all(forward):
         def step(i, run):
-            for h in range(NU):
-                run = near_block(i * NU + h, run, forward)
+            made = [near_product(i * NU + h, forward) for h in range(NU)]
+            for h, (z, cont) in enumerate(made):
+                run = z + cont * run
+                nprod[i * NU + h] = run
             return run
 
         lax.fori_loop(0, NEAR // NU, step, blank)
@@ -298,10 +293,12 @@
 
     run = far_segment(0, blank, False)
     got_x(3)
+    got_side(1)
     far_segment(1, run, False)
-    got_side(1)
+    got_side(2)
     keep[4].wait()
     near_all(False)
+    got_side(3)
 
     def copy(src, dst, k, peer):
         return pltpu.make_async_remote_copy(
@@ -366,6 +363,20 @@
         pair_sum(2, b, n, 1)
         go(mine.at[2, at_b], done_in.at[1, at_b], k + 5, to_down)
 
+    def direct_phase(ph):
+        lo, n = PHASES[ph]
+        at = pl.ds(lo, n)
+        for j, peer, slot in ((0, to_far, 2), (1, to_up, 0), (2, to_down, 1)):
+            arrived(mate_in.at[j, at], 10 * ph + j)
+            pair_sum(j, lo, n)
+            go(mine.at[j, at], done_in.at[slot, at], 10 * ph + 4 + j, peer)
+
+    def close_direct(ph):
+        at = pl.ds(*PHASES[ph])
+        arrived(mate_in.at[3, at], 10 * ph + 3)
+        for j, slot in ((0, 2), (1, 0), (2, 1)):
+            arrived(done_in.at[slot, at], 10 * ph + 4 + j)
+
     def close_phase(ph):
         a, b, n, at_a, at_b, k = halves(ph)
         arrived(mate_in.at[3, pl.ds(*PHASES[ph])], 10 * ph + 3)
@@ -381,116 +392,98 @@
     collect(0, CG, 0, 5, 7)
     collect(CG, 2 * CG, CG, 5, 7)
     to_the_mate(0)
-    got_side(2)
     collect(2 * CG, 3 * CG, -CG, 5, 7)
     to_the_mate(1)
-    open_phase(0)
-    got_side(3)
-    open_phase(1)
     keep[1].wait()
     for i in range(4):
         garrived(xo.at[own, :, cols(mates[i])], 18 + i)
         garrived(xo.at[left_x, :, cols(mates[i])], 22 + i)
         garrived(xo.at[right_x, :, cols(mates[i])], 26 + i)
-
+    open_phase(0)
     run = far_segment(0, blank, True)
+    open_phase(1)
+    far_segment(1, run, True)
     pass_phase(0)
-    far_segment(1, run, True)
+    near_all(True)
     pass_phase(1)
-    near_all(True)
     collect(3 * CG, 4 * CG, -3 * CG, 6, 8)
     to_the_mate(2)
+    direct_phase(2)
     close_phase(0)
 
     def edge(i, carry):
         at = pl.ds(i * chunk, chunk)
-        side_out[at] = whole(at)
+        side_out[at] = whole(at).astype(BF16)
         return carry
 
     lax.fori_loop(0, CG // chunk, edge, 0)
     go(side_out.at[pl.ds(0, CG)], side_in.at[0], 30, to_prev)
     lax.fori_loop(CG // chunk, 2 * CG // chunk, edge, 0)
     go(side_out.at[pl.ds(CG, CG)], side_in.at[1], 31, to_next)
-    open_phase(2)
     close_phase(1)
-    pass_phase(2)
     arrived(side_in.at[0], 30)
     arrived(side_in.at[1], 31)
 
     def own_adjoint(i, carry):
         at = i * chunk
         here = pl.ds(at, chunk)
-        a = whole(pl.ds(2 * CG + at, chunk)) + side_in[0, here] + side_in[1, here]
+        a = whole(pl.ds(2 * CG + at, chunk)) + side_in[0, here].astype(F32) + side_in[1, here].astype(F32)
         adj[here, 0] = a[:, 0]
         adj[here, 1] = -a[:, 1]
         return carry
 
     lax.fori_loop(0, CG // chunk, own_adjoint, 0)
-    close_phase(2)
+    close_direct(2)
 
     def last(i, carry):
         here = pl.ds(i * chunk, chunk)
-        f = whole(pl.ds(3 * CG + i * chunk, chunk))
+        at = pl.ds(3 * CG + i * chunk, chunk)
+        f = whole(at) + done_in[2, at].astype(F32)
         fwd[here] = f
         prd = f[:, 0] * adj[here, 0] - f[:, 1] * adj[here, 1]
-        both = jnp.sum(prd, axis=1) * (1.0 / (MEMBERS * COLS))
-        sens[2 * i] = both[:COLS]
-        sens[2 * i + 1] = both[COLS:]
+        sens[here] = jnp.sum(prd, axis=1) * (1.0 / (MEMBERS * COLS))
         return carry
 
     lax.fori_loop(0, CG // chunk, last, 0)
 
     sent = []
-
-    def spread(src_of, dst, sems_out, sems_in):
-        out = []
-        for off in range(1, MEMBERS):
-            to = (s + off) % MEMBERS
-            d = pltpu.make_async_remote_copy(
-                src_ref=src_of(to), dst_ref=dst.at[off - 1], send_sem=sems_out.at[off - 1],
-                recv_sem=sems_in.at[off - 1], device_id={"sub": to}, device_id_type=MESH,
-            )
-            d.start()
-            out.append(d)
-        sent.extend(out)
-        return out
-
-    for d in spread(lambda to: sens.at[to], sgot, ssend, srecv):
+    for off in range(1, MEMBERS):
+        d = pltpu.make_async_remote_copy(
+            src_ref=sens, dst_ref=sgot.at[off - 1], send_sem=ssend.at[off - 1], recv_sem=srecv.at[off - 1],
+            device_id={"sub": (s + off) % MEMBERS}, device_id_type=MESH,
+        )
+        d.start()
+        sent.append(d)
+    for d in sent:
         d.wait_recv()
-    value = sens[s]
+    value = sens[...]
     for off in range(MEMBERS - 1):
         value = value + sgot[off]
-    counted = counts[pl.ds(pl.multiple_of(4 * s, 4), 4), :]
-    total_grid = None
-    for k in range(2):
-        tops, rests = [], []
-        for h in range(2):
-            j = 2 * k + h
-            at = pl.multiple_of((4 * s + j) * CS, CS)
+    summed[...] = value
+    KU = 4
+
+    def clusters(i, acc):
+        lhs = []
+        for h in range(KU):
+            k = i * KU + h
+            at = pl.multiple_of(k * CS, CS)
+            value, count = summed[pl.ds(k, 1), :], counts[pl.ds(k, 1), :]
+            tops, rests = [], []
             for m in range(4):
-                wt = weights[pl.ds(m, 1), pl.ds(at, CS)]
-                val = wt * value[j : j + 1]
-                val = jnp.where(counted[j : j + 1] > m, val, jnp.zeros_like(val))
+                val = weights[pl.ds(m, 1), pl.ds(at, CS)] * value
+                val = jnp.where(count > m, val, jnp.zeros_like(val))
                 top = val.astype(BF16).astype(F32)
-                lo = (4 * h + m) * CS
-                here = low_hot[k, :, lo : lo + CS]
-                tops.append(here * wide_of(top))
-                rests.append(here * wide_of(val - top))
-        hits = jnp.concatenate([jnp.concatenate(tops, axis=1), jnp.concatenate(rests, axis=1)], axis=0)
-        g = mm(high_hot[k], hits, NT)
-        g = g[:, :CS] + g[:, CS:]
-        total_grid = g if k == 0 else total_grid + g
-    grid[...] = total_grid
-
-    def part_of(member):
-        return grid.at[pl.ds(pl.multiple_of(member * GROUPS, GROUPS), GROUPS)]
-
-    arrivals = spread(part_of, got, psend, precv)
-    all_rows = grid[pl.ds(pl.multiple_of(s * GROUPS, GROUPS), GROUPS), :]
-    for d in arrivals:
-        d.wait_recv()
-    for off in range(MEMBERS - 1):
-        all_rows = all_rows + got[off]
+                hit = high_hot[k, :, m * CS : m * CS + CS]
+                tops.append(hit * wide_of(top, GROUPS))
+                rests.append(hit * wide_of(val - top, GROUPS))
+            lhs.append(jnp.concatenate([jnp.concatenate(tops, axis=1), jnp.concatenate(rests, axis=1)], axis=0))
+        made = [mm(lhs[h], low_hot[i * KU + h], NT) for h in range(KU)]
+        for g in made:
+            acc = acc + g
+        return acc
+
+    both = lax.fori_loop(0, CG // KU, clusters, jnp.zeros((2 * GROUPS, CS), F32))
+    all_rows = both[:GROUPS] + both[GROUPS:]
     for k in range(GROUPS):
         row[k] = all_rows[k : k + 1]
 
@@ -567,15 +560,14 @@
             pltpu.VMEM((4, WIDE) + half, F32),
             pltpu.VMEM((3, WIDE) + half, BF16),
             pltpu.VMEM((2, WIDE) + half, BF16),
-            pltpu.VMEM((2, WIDE) + half, BF16),
-            pltpu.VMEM((2 * CG,) + half, F32),
-            pltpu.VMEM((2, CG) + half, F32),
-            pltpu.VMEM((MEMBERS, COLS, CS), F32),
-            pltpu.VMEM((MEMBERS - 1, COLS, CS), F32),
-            pltpu.VMEM((2, GROUPS * MEMBERS, 8 * CS), BF16),
-            pltpu.VMEM((2, CS, 8 * CS), BF16),
-            pltpu.VMEM((GROUPS * MEMBERS, CS), F32),
-            pltpu.VMEM((MEMBERS - 1, GROUPS, CS), F32),
+            pltpu.VMEM((3, WIDE) + half, BF16),
+            pltpu.VMEM((2 * CG,) + half, BF16),
+            pltpu.VMEM((2, CG) + half, BF16),
+            pltpu.VMEM((CG, CS), F32),
+            pltpu.VMEM((MEMBERS - 1, CG, CS), F32),
+            pltpu.VMEM((CG, CS), F32),
+            pltpu.VMEM((CG, GROUPS, 4 * CS), BF16),
+            pltpu.VMEM((CG, CS, 4 * CS), BF16),
             pltpu.VMEM((GROUPS, 1, CS), F32),
             pltpu.VMEM((GROUPS - 1, 1, CS), F32),
             sems(6),
@@ -583,8 +575,6 @@
             sems(30),
             sems(32),
             sems(32),
-            sems(MEMBERS - 1),
-            sems(MEMBERS - 1),
             sems(MEMBERS - 1),
             sems(MEMBERS - 1),
             sems(GROUPS - 1),

time: 59.2 us -> 57.6 us (0.973)
  Pallas kernels: 58.4 us -> 56.8 us
    pallas_call x1, Pallas kernels: 56.7 us -> 55.1 us  [shards(): pl.pallas_call(kernel, out_shape=(jax.ShapeDtypeStruct((CG,) + half, F32)...]
where the time goes in v4:
time: 57.6 us; the launch traced here: 57.4 us
  Pallas kernels  56.8 us (99%)
  between operations  0.64 us (1%)
    pallas_call x1, Pallas kernels, shards(): pl.pallas_call(kernel, out_shape=(jax.ShapeDtypeStruct((CG,) + half, F32)...  55.1 us
    pallas_call x1, Pallas kernels, shards(): pl.pallas_call(hand_out, out_shape=tuple((jax.ShapeDtypeStruct(a.shape, a...  1.68 us

profile of v4, /device:TPU:1, one launch (start us, length us, event | category | flops | bytes accessed | tf_op | source)
XLA Modules:
  0.0 57.4 jit_solution(937933719739136212)
XLA Ops:
  0.6 55.1 %operator.1 = (f32[32,2,4,128]{3,2,1,0:T(4,128)}, f32[32,2,4,128]{3,2,1,0:T(4,128)}, f32[1,128]{1,0:T(1,128)}) custom-call(bf16[32,2,4,128]{3,2,1,0:T(4,128)(2,1)} %bitcast.15, bf16[32,2,4,128]{3,2,1,0:T(4,128)(2,1)} %bitcast.16, bf16[128,2,32,128]{3,2,1,0:T(8,128)(2,1)} %u_hbm.1, bf16[128,2,32,128]{3,2,1,0:T(8,128)(2,1)} %v_hbm.1, ...), custom_call_target="tpu_custom_call" | custom-call | tf_op jit(solution)/shard_map/operator/pallas_call | solution.py:539
  55.7 1.7 %hand_out.1 = (f32[32,2,4,128]{3,2,1,0:T(4,128)}, f32[32,2,4,128]{3,2,1,0:T(4,128)}, f32[1,128]{1,0:T(1,128)}) custom-call(f32[32,2,4,128]{3,2,1,0:T(4,128)} %get-tuple-element.9.a, f32[32,2,4,128]{3,2,1,0:T(4,128)} %get-tuple-element.10.b, f32[1,128]{1,0:T(1,128)} %get-tuple-element.11.c), custom_call_target="tpu_custom_call" | custom-call | tf_op jit(solution)/shard_map/hand_out/pallas_call | solution.py:589

commit v5 on v4

--- a/solution.py
+++ b/solution.py
@@ -57,7 +57,7 @@
     return pl.ds(pl.multiple_of(COLS * member, COLS), COLS)
 
 
-PHASES = ((0, 2 * CG), (2 * CG, CG), (3 * CG, CG))
+PHASES = ((0, CG), (CG, CG), (2 * CG, CG), (3 * CG, CG))
 
 
 def kernel(
@@ -390,25 +390,28 @@
         return a + done_in[0, at].astype(F32) + done_in[1, at].astype(F32)
 
     collect(0, CG, 0, 5, 7)
+    to_the_mate(0)
     collect(CG, 2 * CG, CG, 5, 7)
-    to_the_mate(0)
+    to_the_mate(1)
     collect(2 * CG, 3 * CG, -CG, 5, 7)
-    to_the_mate(1)
+    to_the_mate(2)
     keep[1].wait()
     for i in range(4):
         garrived(xo.at[own, :, cols(mates[i])], 18 + i)
         garrived(xo.at[left_x, :, cols(mates[i])], 22 + i)
         garrived(xo.at[right_x, :, cols(mates[i])], 26 + i)
     open_phase(0)
+    open_phase(1)
     run = far_segment(0, blank, True)
-    open_phase(1)
+    open_phase(2)
     far_segment(1, run, True)
     pass_phase(0)
+    pass_phase(1)
     near_all(True)
-    pass_phase(1)
+    pass_phase(2)
     collect(3 * CG, 4 * CG, -3 * CG, 6, 8)
-    to_the_mate(2)
-    direct_phase(2)
+    to_the_mate(3)
+    direct_phase(3)
     close_phase(0)
 
     def edge(i, carry):
@@ -417,12 +420,13 @@
         return carry
 
     lax.fori_loop(0, CG // chunk, edge, 0)
-    go(side_out.at[pl.ds(0, CG)], side_in.at[0], 30, to_prev)
+    go(side_out.at[pl.ds(0, CG)], side_in.at[0], 40, to_prev)
+    close_phase(1)
     lax.fori_loop(CG // chunk, 2 * CG // chunk, edge, 0)
-    go(side_out.at[pl.ds(CG, CG)], side_in.at[1], 31, to_next)
-    close_phase(1)
-    arrived(side_in.at[0], 30)
-    arrived(side_in.at[1], 31)
+    go(side_out.at[pl.ds(CG, CG)], side_in.at[1], 41, to_next)
+    close_phase(2)
+    arrived(side_in.at[0], 40)
+    arrived(side_in.at[1], 41)
 
     def own_adjoint(i, carry):
         at = i * chunk
@@ -433,7 +437,7 @@
         return carry
 
     lax.fori_loop(0, CG // chunk, own_adjoint, 0)
-    close_direct(2)
+    close_direct(3)
 
     def last(i, carry):
         here = pl.ds(i * chunk, chunk)
@@ -573,8 +577,8 @@
             sems(6),
             sems(30),
             sems(30),
-            sems(32),
-            sems(32),
+            sems(42),
+            sems(42),
             sems(MEMBERS - 1),
             sems(MEMBERS - 1),
             sems(GROUPS - 1),

time: 57.6 us -> 57.7 us (level)
  no operation moved by 1% of the time
where the time goes in v5:
time: 57.7 us; the launch traced here: 57.5 us
  Pallas kernels  56.9 us (99%)
  between operations  0.64 us (1%)
    pallas_call x1, Pallas kernels, shards(): pl.pallas_call(kernel, out_shape=(jax.ShapeDtypeStruct((CG,) + half, F32)...  55.2 us
    pallas_call x1, Pallas kernels, shards(): pl.pallas_call(hand_out, out_shape=tuple((jax.ShapeDtypeStruct(a.shape, a...  1.68 us

profile of v5, /device:TPU:1, one launch (start us, length us, event | category | flops | bytes accessed | tf_op | source)
XLA Modules:
  0.0 57.5 jit_solution(6846173403175580309)
XLA Ops:
  0.6 55.2 %operator.1 = (f32[32,2,4,128]{3,2,1,0:T(4,128)}, f32[32,2,4,128]{3,2,1,0:T(4,128)}, f32[1,128]{1,0:T(1,128)}) custom-call(bf16[32,2,4,128]{3,2,1,0:T(4,128)(2,1)} %bitcast.15, bf16[32,2,4,128]{3,2,1,0:T(4,128)(2,1)} %bitcast.16, bf16[128,2,32,128]{3,2,1,0:T(8,128)(2,1)} %u_hbm.1, bf16[128,2,32,128]{3,2,1,0:T(8,128)(2,1)} %v_hbm.1, ...), custom_call_target="tpu_custom_call" | custom-call | tf_op jit(solution)/shard_map/operator/pallas_call | solution.py:543
  55.9 1.7 %hand_out.1 = (f32[32,2,4,128]{3,2,1,0:T(4,128)}, f32[32,2,4,128]{3,2,1,0:T(4,128)}, f32[1,128]{1,0:T(1,128)}) custom-call(f32[32,2,4,128]{3,2,1,0:T(4,128)} %get-tuple-element.9.a, f32[32,2,4,128]{3,2,1,0:T(4,128)} %get-tuple-element.10.b, f32[1,128]{1,0:T(1,128)} %get-tuple-element.11.c), custom_call_target="tpu_custom_call" | custom-call | tf_op jit(solution)/shard_map/hand_out/pallas_call | solution.py:593
